TPU v7x, 32 devices: a whole 2x2x4 slice. The times are simulated.
32 devices in a mesh: tx: 4 (over z), cell: 8 (over y, x, core).
Axes of the slice: x: 2, y: 2, z: 4, core: 2. Of those that a mesh axis runs over, the one named last changes fastest.
Arguments:
- currents: bfloat16 [2, 2, 8192, 4096], P(None, None, 'cell', 'tx'), may hold values from -6 to 6
- green: bfloat16 [2, 2, 64, 8192], P(None, None, 'tx', 'cell'), may hold values from -0.0625 to 0.0625
- angular_freq: float32 [2], replicated, may hold values from 0.5 to 3
- gate_time: float32 [64], replicated, may hold values from 0.1 to 3
Outputs:
- gated: float32 [64, 64, 4096], P(None, 'cell', 'tx')
All inputs are finite; a program needn't handle non-finite values.
Results may differ from a plain program's by a relative error of at most 0.0003.
Values may be sent and summed in bfloat16 or wider, within the bound.
No kernel may reach another device: no remote copies, remote signals or barrier semaphores. Data moves between devices by JAX's collectives and lax.ppermute only.
A program may use at most 128 MiB of HBM per device.

v0:
```python
import jax
import jax.numpy as jnp
from jax import lax
from jax.sharding import PartitionSpec as P


def complex_rows(green_block, currents):
    real_list = []
    imag_list = []
    for which_freq in range(currents.shape[1]):
        green_real = green_block[0, which_freq]
        green_imag = green_block[1, which_freq]
        curr_real = currents[0, which_freq]
        curr_imag = currents[1, which_freq]
        real_list.append(
            jnp.dot(green_real, curr_real, preferred_element_type=jnp.float32)
            - jnp.dot(green_imag, curr_imag, preferred_element_type=jnp.float32)
        )
        imag_list.append(
            jnp.dot(green_real, curr_imag, preferred_element_type=jnp.float32)
            + jnp.dot(green_imag, curr_real, preferred_element_type=jnp.float32)
        )
    return jnp.stack([jnp.stack(real_list), jnp.stack(imag_list)])


def per_device(currents, green, angular_freq, gate_time):
    gate_phase = gate_time[:, None] * angular_freq[None, :]
    cosine_weight = jnp.cos(gate_phase)
    sine_weight = jnp.sin(gate_phase)
    all_green = lax.all_gather(green, "tx", axis=2, tiled=True)
    receiver_portions = lax.psum_scatter(
        jnp.moveaxis(complex_rows(all_green, currents), 2, 0),
        "cell",
        scatter_dimension=0,
        tiled=True,
    )
    gated = jnp.einsum(
        "qc,ncm->qnm", cosine_weight, receiver_portions[:, 0], precision=lax.Precision.HIGHEST
    )
    gated = gated - jnp.einsum(
        "qc,ncm->qnm", sine_weight, receiver_portions[:, 1], precision=lax.Precision.HIGHEST
    )
    return gated


def solution(mesh):
    return jax.shard_map(
        per_device,
        mesh=mesh,
        in_specs=(P(None, None, "cell", "tx"), P(None, None, "tx", "cell"), P(), P()),
        out_specs=P(None, "cell", "tx"),
        check_vma=False,
    )
```

profile of v0, /device:TPU:0, one launch (start us, length us, event | category | flops | bytes accessed | tf_op | source)
XLA Modules:
  0.0 88.4 jit_solution(19578362142502962)
XLA Ops:
  6.5 0.0 reduce-scatter.2.cloned.1.call-start
  6.5 17.6 %all_gather.3 = bf16[2,2,64,1024]{3,2,1,0:T(8,128)(2,1)S(1)} all-gather(bf16[2,2,16,1024]{3,2,1,0:T(8,128)(2,1)} %param.5), channel_id=1, replica_groups=mesh['tx'=4,'cell'=8] {'tx'}, dimensions={2}, use_global_device_ids=true | all-gather | bytes 655360 | tf_op jit(solution)/shard_map/all_gather | solution.py:30
  24.1 0.0 copy-start
  24.1 2.2 %fusion = f32[64,1024]{1,0:T(8,128)S(1)} fusion(bf16[2,2,1024,1024]{3,2,1,0:T(8,128)(2,1)} %param.4, bf16[2,2,64,1024]{3,2,1,0:T(8,128)(2,1)S(1)} %all_gather.3), kind=kOutput, calls=%fused_computation | convolution fusion | flops 134217728 | bytes 2490368 | tf_op jit(solution)/shard_map/dot_general | solution.py:20
  26.3 2.5 %fusion.8 = f32[64,1024]{1,0:T(8,128)S(1)} fusion(bf16[2,2,1024,1024]{3,2,1,0:T(8,128)(2,1)} %param.4, bf16[2,2,64,1024]{3,2,1,0:T(8,128)(2,1)S(1)} %all_gather.3), kind=kOutput, calls=%fused_computation.8 | convolution fusion | flops 134217728 | bytes 2490368 | tf_op jit(solution)/shard_map/dot_general | solution.py:20
  28.8 2.1 %fusion.2 = f32[64,1024]{1,0:T(8,128)S(1)} fusion(bf16[2,2,1024,1024]{3,2,1,0:T(8,128)(2,1)} %param.4, bf16[2,2,64,1024]{3,2,1,0:T(8,128)(2,1)S(1)} %all_gather.3), kind=kOutput, calls=%fused_computation.2 | convolution fusion | flops 134217728 | bytes 2490368 | tf_op jit(solution)/shard_map/dot_general | solution.py:17
  30.9 2.1 %fusion.10 = f32[64,1024]{1,0:T(8,128)S(1)} fusion(bf16[2,2,1024,1024]{3,2,1,0:T(8,128)(2,1)} %param.4, bf16[2,2,64,1024]{3,2,1,0:T(8,128)(2,1)S(1)} %all_gather.3), kind=kOutput, calls=%fused_computation.10 | convolution fusion | flops 134217728 | bytes 2490368 | tf_op jit(solution)/shard_map/dot_general | solution.py:17
  33.0 0.0 copy-done
  33.0 0.5 fusion.45
  33.5 0.5 fusion.33
  34.0 0.5 fusion.39
  34.5 0.5 fusion.27
  35.0 0.1 maximum_bitcast_fusion.1
  35.0 0.0 copy-start.1
  35.0 0.0 copy-start.2
  35.1 1.1 %maximum_bitcast_fusion = f32[64,2,2,1024]{3,0,2,1:T(8,128)} fusion(f32[1,2,64,1024]{3,2,1,0:T(8,128)S(1)} %get-tuple-element.8, f32[1,2,64,1024]{3,2,1,0:T(8,128)S(1)} %get-tuple-element.7), kind=kLoop, calls=%fused_computation.33 | loop fusion | flops 262144 | bytes 2097152 | tf_op jit(solution)/shard_map/transpose | solution.py:32
  36.1 0.0 reduce-scatter.2.cloned.1.call-update
  36.2 38.0 %reduce-scatter.2.cloned.1.call-done = f32[8,2,2,1024]{3,0,2,1:T(8,128)} async-done(((f32[64,2,2,1024]{3,0,2,1:T(8,128)}), f32[8,2,2,1024]{3,0,2,1:T(8,128)}) %reduce-scatter.2.cloned.1.call-update) | async-done | bytes 131088 | tf_op jit(solution)/shard_map/reduce_scatter | solution.py:31
  74.1 0.9 slice_bitcast_fusion.12
  75.0 0.0 copy-done.1
  75.0 0.0 copy-done.2
  75.0 2.0 %fusion.49 = f32[64,8,1024]{2,0,1:T(8,128)S(1)} fusion(f32[8,2,1024]{2,0,1:T(8,128)S(1)} %get-tuple-element.6, f32[64]{0:T(128)S(1)} %copy-done.1, f32[2]{0:T(128)S(1)} %copy-done.2), kind=kOutput, calls=%fused_computation.43 | convolution fusion | flops 12583040 | bytes 2162952 | tf_op jit(solution)/shard_map/qc,ncm->qnm/dot_general | solution.py:37
  77.0 2.0 %convolution_subtract_fusion = f32[64,8,1024]{2,0,1:T(8,128)S(1)} fusion(f32[64,8,1024]{2,0,1:T(8,128)S(1)} %fusion.49, f32[8,2,1024]{2,0,1:T(8,128)S(1)} %get-tuple-element.5, f32[64]{0:T(128)S(1)} %copy-done.1, f32[2]{0:T(128)S(1)} %copy-done.2), kind=kOutput, calls=%fused_computation.24 | convolution fusion | flops 13107328 | bytes 4260104 | tf_op jit(solution)/shard_map/qc,ncm->qnm/dot_general | solution.py:40
  79.0 2.5 %copy.7 = f32[64,8,1024]{2,1,0:T(8,128)} copy(f32[64,8,1024]{2,0,1:T(8,128)S(1)} %convolution_subtract_fusion) | data formatting | bytes 4194304 | tf_op jit(solution)/shard_map/sub | solution.py:40
Async XLA Ops:
  6.5 67.6 %reduce-scatter.2.cloned.1.call-start = ((), (), s32[]{:S(2)}) async-start(), calls=%async_computation.1 | async-start | bytes 1179648 | tf_op jit(solution)/shard_map/reduce_scatter | solution.py:31
  24.1 8.9 %copy-start = (bf16[2,2,1024,1024]{3,2,1,0:T(8,128)(2,1)S(1)}, bf16[2,2,1024,1024]{3,2,1,0:T(8,128)(2,1)}, u32[]{:S(2)}) copy-start(bf16[2,2,1024,1024]{3,2,1,0:T(8,128)(2,1)} %param.4) | copy-start | bytes 25165828
  35.0 40.0 %copy-start.1 = (f32[64]{0:T(128)S(1)}, f32[64]{0:T(128)}, u32[]{:S(2)}) copy-start(f32[64]{0:T(128)} %param.7) | copy-start | bytes 772
  35.0 40.0 %copy-start.2 = (f32[2]{0:T(128)S(1)}, f32[2]{0:T(128)}, u32[]{:S(2)}) copy-start(f32[2]{0:T(128)} %param.6) | copy-start | bytes 28
Sparse Core Ops, SparseCore 0:
  36.3 37.7 reduce-scatter.1
where the time goes:
time: 88.6 us; the launch traced here: 88.4 us
  waiting for transfers between devices  38 us (43%)
  blocking collectives  17.6 us (20%)
  matrix products  14.8 us (17%)
  between operations  13.5 us (15%)
  local copies, waits for them, and re-layouts  3.43 us (4%)
  other arithmetic  1.16 us (1%)
    reduce_scatter x1, waiting for transfers between devices, per_device(): lax.psum_scatter(jnp.moveaxis(complex_rows(all_green, currents), 2, 0), '...  38 us
    all_gather x1, blocking collectives, per_device(): all_green = lax.all_gather(green, 'tx', axis=2, tiled=True)  17.6 us
    dot_general x2, matrix products, complex_rows(): jnp.dot(green_real, curr_imag, preferred_element_type=jnp.float32)  4.73 us
    dot_general x2, matrix products, complex_rows(): jnp.dot(green_imag, curr_imag, preferred_element_type=jnp.float32)  4.14 us
    sub x1, local copies, waits for them, and re-layouts, per_device(): gated - jnp.einsum('qc,ncm->qnm', sine_weight, receiver_portions[:, 1], p...  2.54 us
    dot_general x1, matrix products, per_device(): jnp.einsum('qc,ncm->qnm', sine_weight, receiver_portions[:, 1], precision...  2.02 us
    dot_general x1, matrix products, per_device(): jnp.einsum('qc,ncm->qnm', cosine_weight, receiver_portions[:, 0], precisi...  1.96 us
  transfers between devices with their start and end apart: 1, of which 1 were waited for; matrix products, arithmetic and copies ran while one was open for 0% of the time, Pallas kernels for 0%

commit v1 on v0

v1 whole, which is shorter than its diff:
```python
import functools

import jax
import jax.numpy as jnp
from jax import lax
from jax.experimental import pallas as pl
from jax.experimental.pallas import tpu as pltpu
from jax.sharding import PartitionSpec as P

VMEM = pl.BlockSpec(memory_space=pltpu.VMEM)
SMEM = pl.BlockSpec(memory_space=pltpu.SMEM)
GATES_AT_ONCE = 8


def response_kernel(blocks, chips, place_ref, *refs):
    slots, currents_ref = refs[:blocks], refs[blocks]
    keep_ref, send_ref, straight_ref, crossed_ref = refs[blocks + 1 :]
    my_tx, my_chip, my_core = place_ref[0], place_ref[1], place_ref[2]
    freqs = currents_ref.shape[1]
    per_block = chips // blocks
    rows = slots[0].shape[2] // per_block
    half = rows // 2
    for f in range(freqs):
        for slot in range(blocks):
            block = lax.bitwise_xor(my_tx, slot)
            for j in range(per_block):
                chip = lax.bitwise_xor(block * per_block + j, my_chip)
                real = slots[slot][0, f, j * rows : (j + 1) * rows, :]
                imag = slots[slot][1, f, j * rows : (j + 1) * rows, :]
                straight_ref[f, 0, chip] = real
                straight_ref[f, 1, chip] = imag
                crossed_ref[f, 0, chip] = -imag
                crossed_ref[f, 1, chip] = real
    cells = currents_ref.shape[2]
    width = currents_ref.shape[3]
    step = min(width, 512)
    for f in range(freqs):
        straight = straight_ref[f].reshape(2 * chips * rows, cells)
        crossed = crossed_ref[f].reshape(2 * chips * rows, cells)
        for at in range(0, width, step):
            cols = slice(at, at + step)
            total = jnp.dot(straight, currents_ref[0, f, :, cols], preferred_element_type=jnp.float32)
            total += jnp.dot(crossed, currents_ref[1, f, :, cols], preferred_element_type=jnp.float32)
            total = total.reshape(2, chips, 2, half, step)
            first = my_core == 0
            for part in range(2):
                keep = jnp.where(first, total[part, :, 0], total[part, :, 1])
                send = jnp.where(first, total[part, :, 1], total[part, :, 0])
                keep_ref[:, f * 2 + part, :, cols] = keep
                send_ref[:, f * 2 + part, :, cols] = send


def responses(place, slots, currents, chips):
    _, freqs, block_rows, cells = slots[0].shape
    width = currents.shape[3]
    rows = block_rows * len(slots) // chips
    out = jax.ShapeDtypeStruct((chips, 2 * freqs, rows // 2, width), jnp.float32)
    products = pltpu.VMEM((freqs, 2, chips, rows, cells), jnp.bfloat16)
    return pl.pallas_call(
        functools.partial(response_kernel, len(slots), chips),
        out_shape=(out, out),
        in_specs=[SMEM] + [VMEM] * (len(slots) + 1),
        out_specs=(VMEM, VMEM),
        scratch_shapes=[products, products],
        compiler_params=pltpu.CompilerParams(vmem_limit_bytes=48 << 20),
        name="responses",
    )(place, *slots, currents)


def gate_kernel(parts, weight_ref, *refs):
    pieces, out_ref = refs[:parts], refs[parts]
    held_ref, sems = refs[parts + 1 :]
    terms = pieces[0].shape[0]
    gates = out_ref.shape[0]
    total = [sum(piece[t] for piece in pieces[1:]) + pieces[0][t] for t in range(terms)]
    copies = []
    for at in range(0, gates, GATES_AT_ONCE):
        for g in range(at, at + GATES_AT_ONCE):
            value = weight_ref[0, g] * total[0]
            for t in range(1, terms):
                value += weight_ref[t, g] * total[t]
            held_ref[g] = value
        group = pl.ds(at, GATES_AT_ONCE)
        copy = pltpu.make_async_copy(held_ref.at[group], out_ref.at[group], sems.at[at // GATES_AT_ONCE])
        copy.start()
        copies.append(copy)
    for copy in copies:
        copy.wait()


def gates_of(weights, pieces):
    terms, gates = weights.shape
    _, rows, width = pieces[0].shape
    return pl.pallas_call(
        functools.partial(gate_kernel, len(pieces)),
        out_shape=jax.ShapeDtypeStruct((gates, rows, width), jnp.float32),
        in_specs=[SMEM] + [VMEM] * len(pieces),
        out_specs=pl.BlockSpec(memory_space=pl.ANY),
        scratch_shapes=[
            pltpu.VMEM((gates, rows, width), jnp.float32),
            pltpu.SemaphoreType.DMA((gates // GATES_AT_ONCE,)),
        ],
        compiler_params=pltpu.CompilerParams(vmem_limit_bytes=32 << 20),
        name="gates",
    )(weights, *pieces)


def per_device(txs, cells, currents, green, angular_freq, gate_time):
    chips = cells // 2
    my_cell = lax.axis_index("cell")
    place = jnp.stack([lax.axis_index("tx"), my_cell // 2, my_cell % 2]).astype(jnp.int32)
    gate_phase = angular_freq[:, None] * gate_time[None, :]
    weights = jnp.stack([jnp.cos(gate_phase), -jnp.sin(gate_phase)], 1).reshape(-1, gate_time.shape[0])

    slots = [green] + [lax.ppermute(green, "tx", [(i, i ^ s) for i in range(txs)]) for s in range(1, txs)]
    keep, send = responses(place, slots, currents, chips)
    chip_sum = keep + lax.ppermute(send, "cell", [(i, i ^ 1) for i in range(cells)])
    pieces = [chip_sum[0]] + [
        lax.ppermute(chip_sum[k], "cell", [(i, i ^ (2 * k)) for i in range(cells)]) for k in range(1, chips)
    ]
    return gates_of(weights, pieces)


def solution(mesh):
    return jax.shard_map(
        functools.partial(per_device, mesh.shape["tx"], mesh.shape["cell"]),
        mesh=mesh,
        in_specs=(P(None, None, "cell", "tx"), P(None, None, "tx", "cell"), P(), P()),
        out_specs=P(None, "cell", "tx"),
        check_vma=False,
    )
```

time: 88.6 us -> 34.2 us (0.39)
  waiting for transfers between devices: 38 us -> 16.5 us
  blocking collectives: 17.6 us -> 0 us
  matrix products: 14.8 us -> 0 us
  between operations: 13.5 us -> 0.06 us
  starting transfers between devices: 0.01 us -> 9.24 us
  Pallas kernels: 0 us -> 6.71 us
  local copies, waits for them, and re-layouts: 3.43 us -> 0.95 us
  other arithmetic: 1.16 us -> 0.25 us
    reduce_scatter x1 -> x0, waiting for transfers between devices: 38 us -> none  [per_device(): lax.psum_scatter(jnp.moveaxis(complex_rows(all_green, currents), 2, 0), '...]
    all_gather x1 -> x0, blocking collectives: 17.6 us -> none  [per_device(): all_green = lax.all_gather(green, 'tx', axis=2, tiled=True)]
    ppermute x0 -> x7, waiting for transfers between devices: none -> 16.5 us  [the longest x3 8.88 us: per_device(): lax.ppermute(green, 'tx', [(i, i ^ s) for i in range(txs)])]
    dot_general x10 -> x0, matrix products: 14.8 us -> none  [the longest x2 4.73 us: complex_rows(): jnp.dot(green_real, curr_imag, preferred_element_type=jnp.float32)]
    ppermute x0 -> x7, starting transfers between devices: none -> 9.24 us  [the longest x3 5.62 us: per_device(): lax.ppermute(green, 'tx', [(i, i ^ s) for i in range(txs)])]
    pallas_call x0 -> x2, Pallas kernels: none -> 6.71 us  [the longest x1 4.69 us: responses(): pl.pallas_call(functools.partial(response_kernel, len(slots), chips), out...]
    sub x1 -> x0, local copies, waits for them, and re-layouts: 2.54 us -> none  [per_device(): gated - jnp.einsum('qc,ncm->qnm', sine_weight, receiver_portions[:, 1], p...]
    transpose x1 -> x0, other arithmetic: 1.08 us -> none  [per_device(): jnp.moveaxis(complex_rows(all_green, currents), 2, 0)]
  transfers between devices with their start and end apart: 1 -> 7, of which waited for: 1 -> 6; matrix products, arithmetic and copies ran while one was open for 0% -> 1% of each run, Pallas kernels for 0% -> 0%
where the time goes in v1:
time: 34.2 us; the launch traced here: 33.7 us
  waiting for transfers between devices  16.5 us (48%)
  starting transfers between devices  9.24 us (27%)
  Pallas kernels  6.71 us (20%)
  local copies, waits for them, and re-layouts  0.95 us (3%)
    ppermute x3, waiting for transfers between devices, per_device(): lax.ppermute(green, 'tx', [(i, i ^ s) for i in range(txs)])  8.88 us
    ppermute x3, waiting for transfers between devices, per_device(): lax.ppermute(chip_sum[k], 'cell', [(i, i ^ 2 * k) for i in range(cells)])  5.7 us
    ppermute x3, starting transfers between devices, per_device(): lax.ppermute(green, 'tx', [(i, i ^ s) for i in range(txs)])  5.62 us
    pallas_call x1, Pallas kernels, responses(): pl.pallas_call(functools.partial(response_kernel, len(slots), chips), out...  4.69 us
    ppermute x3, starting transfers between devices, per_device(): lax.ppermute(chip_sum[k], 'cell', [(i, i ^ 2 * k) for i in range(cells)])  3.55 us
    pallas_call x1, Pallas kernels, gates_of(): pl.pallas_call(functools.partial(gate_kernel, len(pieces)), out_shape=jax...  2.02 us
    ppermute x1, waiting for transfers between devices, per_device(): lax.ppermute(send, 'cell', [(i, i ^ 1) for i in range(cells)])  1.9 us
    unnamed x6, local copies, waits for them, and re-layouts  0.91 us
  transfers between devices with their start and end apart: 7, of which 6 were waited for; matrix products, arithmetic and copies ran while one was open for 1% of the time, Pallas kernels for 0%

profile of v1, /device:TPU:0, one launch (start us, length us, event | category | flops | bytes accessed | tf_op | source)
XLA Modules:
  0.0 33.7 jit_solution(10661740643759414019)
XLA Ops:
  0.0 0.0 copy-start.1
  0.0 0.0 copy-start.2
  0.0 4.0 %collective-permute-start.1 = (bf16[2,2,16,1024]{3,2,1,0:T(8,128)(2,1)}, bf16[2,2,16,1024]{3,2,1,0:T(8,128)(2,1)S(1)}, u32[]{:S(2)}, u32[]{:S(2)}) collective-permute-start(bf16[2,2,16,1024]{3,2,1,0:T(8,128)(2,1)} %refs_0_.1), channel_id=1, source_target_pairs={{0,16},{8,24},{16,0},{24,8},{1,17},{9,25},{17,1},{25,9},{2,18},{10... | collective-permute-start | bytes 393224 | tf_op jit(solution)/shard_map/ppermute | solution.py:115
  4.0 1.6 %collective-permute-start = (bf16[2,2,16,1024]{3,2,1,0:T(8,128)(2,1)}, bf16[2,2,16,1024]{3,2,1,0:T(8,128)(2,1)S(1)}, u32[]{:S(2)}, u32[]{:S(2)}) collective-permute-start(bf16[2,2,16,1024]{3,2,1,0:T(8,128)(2,1)} %refs_0_.1), channel_id=1, source_target_pairs={{0,8},{8,0},{16,24},{24,16},{1,9},{9,1},{17,25},{25,17},{2,10},{10... | collective-permute-start | bytes 393224 | tf_op jit(solution)/shard_map/ppermute | solution.py:115
  5.6 0.0 collective-permute-start.2
  5.6 0.1 pad_add_fusion.place_ref
  5.7 6.5 %collective-permute-done.1.refs_2_ = bf16[2,2,16,1024]{3,2,1,0:T(8,128)(2,1)S(1)} collective-permute-done((bf16[2,2,16,1024]{3,2,1,0:T(8,128)(2,1)}, bf16[2,2,16,1024]{3,2,1,0:T(8,128)(2,1)S(1)}, u32[]{:S(2)}, u32[]{:S(2)}) %collective-permute-start.1) | collective-permute-done | bytes 131104 | tf_op jit(solution)/shard_map/ppermute | solution.py:115
  12.2 0.0 collective-permute-done.refs_1_
  12.2 2.4 %collective-permute-done.2.refs_3_ = bf16[2,2,16,1024]{3,2,1,0:T(8,128)(2,1)S(1)} collective-permute-done((bf16[2,2,16,1024]{3,2,1,0:T(8,128)(2,1)}, bf16[2,2,16,1024]{3,2,1,0:T(8,128)(2,1)S(1)}, u32[]{:S(2)}, u32[]{:S(2)}) %collective-permute-start.2) | collective-permute-done | bytes 131104 | tf_op jit(solution)/shard_map/ppermute | solution.py:115
  14.6 0.0 copy-start
  14.6 0.9 %copy-done = bf16[2,2,16,1024]{3,2,1,0:T(8,128)(2,1)S(1)} copy-done((bf16[2,2,16,1024]{3,2,1,0:T(8,128)(2,1)S(1)}, bf16[2,2,16,1024]{3,2,1,0:T(8,128)(2,1)}, u32[]{:S(2)}) %copy-start) | copy-done | bytes 131096
  15.5 4.7 %responses.1 = (f32[4,4,8,1024]{3,2,1,0:T(8,128)S(1)}, f32[4,4,8,1024]{3,2,1,0:T(8,128)S(1)}) custom-call(s32[3]{0:T(128)S(1)} %pad_add_fusion.place_ref, bf16[2,2,16,1024]{3,2,1,0:T(8,128)(2,1)S(1)} %copy-done, bf16[2,2,16,1024]{3,2,1,0:T(8,128)(2,1)S(1)} %collective-permute-done.refs_1_, bf16[2,2,16,1024]{3,2,1,0:T(8,128)(2,1)S(1)} %collective-permute-done.1.refs_2_, ...), custom_call_target="tpu_custom_call" | custom-call | tf_op jit(solution)/shard_map/responses/pallas_call | solution.py:59
  20.2 0.1 collective-permute-start.3
  20.3 1.9 %collective-permute-done.3 = f32[4,4,8,1024]{3,2,1,0:T(8,128)S(1)} collective-permute-done((f32[4,4,8,1024]{3,2,1,0:T(8,128)S(1)}, f32[4,4,8,1024]{3,2,1,0:T(8,128)S(1)}, u32[]{:S(2)}, u32[]{:S(2)}) %collective-permute-start.3) | collective-permute-done | bytes 524320 | tf_op jit(solution)/shard_map/ppermute | solution.py:117
  22.2 0.1 add.9
  22.3 2.5 %collective-permute-start.6 = (f32[4,8,1024]{2,1,0:T(8,128)S(1)}, f32[4,8,1024]{2,1,0:T(8,128)S(1)}, u32[]{:S(2)}, u32[]{:S(2)}) collective-permute-start(f32[4,8,1024]{2,1,0:T(8,128)S(1)} %get-tuple-element.9), channel_id=1, source_target_pairs={{0,6},{1,7},{2,4},{3,5},{4,2},{5,3},{6,0},{7,1},{8,14},{9,15},{10,... | collective-permute-start | bytes 393224 | tf_op jit(solution)/shard_map/ppermute | solution.py:119
  24.8 0.5 %collective-permute-start.5 = (f32[4,8,1024]{2,1,0:T(8,128)S(1)}, f32[4,8,1024]{2,1,0:T(8,128)S(1)}, u32[]{:S(2)}, u32[]{:S(2)}) collective-permute-start(f32[4,8,1024]{2,1,0:T(8,128)S(1)} %get-tuple-element.10), channel_id=1, source_target_pairs={{0,4},{1,5},{2,6},{3,7},{4,0},{5,1},{6,2},{7,3},{8,12},{9,13},{10,... | collective-permute-start | bytes 393224 | tf_op jit(solution)/shard_map/ppermute | solution.py:119
  25.3 0.5 %collective-permute-start.4 = (f32[4,8,1024]{2,1,0:T(8,128)S(1)}, f32[4,8,1024]{2,1,0:T(8,128)S(1)}, u32[]{:S(2)}, u32[]{:S(2)}) collective-permute-start(f32[4,8,1024]{2,1,0:T(8,128)S(1)} %get-tuple-element.11), channel_id=1, source_target_pairs={{0,2},{1,3},{2,0},{3,1},{4,6},{5,7},{6,4},{7,5},{8,10},{9,11},{10,... | collective-permute-start | bytes 393224 | tf_op jit(solution)/shard_map/ppermute | solution.py:119
  25.8 0.0 copy-done.1
  25.8 0.0 copy-done.2
  25.8 0.1 multiply_cosine_fusion
  26.0 3.1 %collective-permute-done.6.refs_3_ = f32[4,8,1024]{2,1,0:T(8,128)S(1)} collective-permute-done((f32[4,8,1024]{2,1,0:T(8,128)S(1)}, f32[4,8,1024]{2,1,0:T(8,128)S(1)}, u32[]{:S(2)}, u32[]{:S(2)}) %collective-permute-start.6) | collective-permute-done | bytes 131104 | tf_op jit(solution)/shard_map/ppermute | solution.py:119
  29.1 2.5 %collective-permute-done.5.refs_2_ = f32[4,8,1024]{2,1,0:T(8,128)S(1)} collective-permute-done((f32[4,8,1024]{2,1,0:T(8,128)S(1)}, f32[4,8,1024]{2,1,0:T(8,128)S(1)}, u32[]{:S(2)}, u32[]{:S(2)}) %collective-permute-start.5) | collective-permute-done | bytes 131104 | tf_op jit(solution)/shard_map/ppermute | solution.py:119
  31.6 0.1 collective-permute-done.4.refs_1_
  31.7 2.0 %gates.1 = f32[64,8,1024]{2,1,0:T(8,128)} custom-call(f32[4,64]{1,0:T(4,128)S(1)} %bitcast.12, f32[4,8,1024]{2,1,0:T(8,128)S(1)} %get-tuple-element.12.refs_0_, f32[4,8,1024]{2,1,0:T(8,128)S(1)} %collective-permute-done.4.refs_1_, f32[4,8,1024]{2,1,0:T(8,128)S(1)} %collective-permute-done.5.refs_2_, f32[4,8,1024]{2,1,0:T(8,128)S(1)} %collective-permute-done.6.refs_3_), custom_call_target="tpu_custom_call" | custom-call | tf_op jit(solution)/shard_map/gates/pallas_call | solution.py:94
  (3 shorter events, 0.0 us)
Async XLA Ops:
  0.0 25.8 %copy-start.1 = (f32[64]{0:T(128)S(1)}, f32[64]{0:T(128)}, u32[]{:S(2)}) copy-start(f32[64]{0:T(128)} %param.7) | copy-start | bytes 772
  0.0 25.8 %copy-start.2 = (f32[2]{0:T(128)S(1)}, f32[2]{0:T(128)}, u32[]{:S(2)}) copy-start(f32[2]{0:T(128)} %param.6) | copy-start | bytes 28
  0.0 12.2 %collective-permute-start.1 = (bf16[2,2,16,1024]{3,2,1,0:T(8,128)(2,1)}, bf16[2,2,16,1024]{3,2,1,0:T(8,128)(2,1)S(1)}, u32[]{:S(2)}, u32[]{:S(2)}) collective-permute-start(bf16[2,2,16,1024]{3,2,1,0:T(8,128)(2,1)} %refs_0_.1), channel_id=1, source_target_pairs={{0,16},{8,24},{16,0},{24,8},{1,17},{9,25},{17,1},{25,9},{2,18},{10... | collective-permute-start | bytes 393224 | tf_op jit(solution)/shard_map/ppermute | solution.py:115
  4.0 8.2 %collective-permute-start = (bf16[2,2,16,1024]{3,2,1,0:T(8,128)(2,1)}, bf16[2,2,16,1024]{3,2,1,0:T(8,128)(2,1)S(1)}, u32[]{:S(2)}, u32[]{:S(2)}) collective-permute-start(bf16[2,2,16,1024]{3,2,1,0:T(8,128)(2,1)} %refs_0_.1), channel_id=1, source_target_pairs={{0,8},{8,0},{16,24},{24,16},{1,9},{9,1},{17,25},{25,17},{2,10},{10... | collective-permute-start | bytes 393224 | tf_op jit(solution)/shard_map/ppermute | solution.py:115
  5.6 9.0 %collective-permute-start.2 = (bf16[2,2,16,1024]{3,2,1,0:T(8,128)(2,1)}, bf16[2,2,16,1024]{3,2,1,0:T(8,128)(2,1)S(1)}, u32[]{:S(2)}, u32[]{:S(2)}) collective-permute-start(bf16[2,2,16,1024]{3,2,1,0:T(8,128)(2,1)} %refs_0_.1), channel_id=1, source_target_pairs={{0,24},{8,16},{16,8},{24,0},{1,25},{9,17},{17,9},{25,1},{2,26},{10... | collective-permute-start | bytes 393224 | tf_op jit(solution)/shard_map/ppermute | solution.py:115
  14.6 0.9 %copy-start = (bf16[2,2,16,1024]{3,2,1,0:T(8,128)(2,1)S(1)}, bf16[2,2,16,1024]{3,2,1,0:T(8,128)(2,1)}, u32[]{:S(2)}) copy-start(bf16[2,2,16,1024]{3,2,1,0:T(8,128)(2,1)} %refs_0_.1) | copy-start | bytes 393220
  20.2 2.0 %collective-permute-start.3 = (f32[4,4,8,1024]{3,2,1,0:T(8,128)S(1)}, f32[4,4,8,1024]{3,2,1,0:T(8,128)S(1)}, u32[]{:S(2)}, u32[]{:S(2)}) collective-permute-start(f32[4,4,8,1024]{3,2,1,0:T(8,128)S(1)} %get-tuple-element.8), channel_id=1, source_target_pairs={{0,1},{1,0},{2,3},{3,2},{4,5},{5,4},{6,7},{7,6},{8,9},{9,8},{10,11... | collective-permute-start | bytes 1572872 | tf_op jit(solution)/shard_map/ppermute | solution.py:117
  22.3 6.8 %collective-permute-start.6 = (f32[4,8,1024]{2,1,0:T(8,128)S(1)}, f32[4,8,1024]{2,1,0:T(8,128)S(1)}, u32[]{:S(2)}, u32[]{:S(2)}) collective-permute-start(f32[4,8,1024]{2,1,0:T(8,128)S(1)} %get-tuple-element.9), channel_id=1, source_target_pairs={{0,6},{1,7},{2,4},{3,5},{4,2},{5,3},{6,0},{7,1},{8,14},{9,15},{10,... | collective-permute-start | bytes 393224 | tf_op jit(solution)/shard_map/ppermute | solution.py:119
  24.8 6.8 %collective-permute-start.5 = (f32[4,8,1024]{2,1,0:T(8,128)S(1)}, f32[4,8,1024]{2,1,0:T(8,128)S(1)}, u32[]{:S(2)}, u32[]{:S(2)}) collective-permute-start(f32[4,8,1024]{2,1,0:T(8,128)S(1)} %get-tuple-element.10), channel_id=1, source_target_pairs={{0,4},{1,5},{2,6},{3,7},{4,0},{5,1},{6,2},{7,3},{8,12},{9,13},{10,... | collective-permute-start | bytes 393224 | tf_op jit(solution)/shard_map/ppermute | solution.py:119
  25.3 6.4 %collective-permute-start.4 = (f32[4,8,1024]{2,1,0:T(8,128)S(1)}, f32[4,8,1024]{2,1,0:T(8,128)S(1)}, u32[]{:S(2)}, u32[]{:S(2)}) collective-permute-start(f32[4,8,1024]{2,1,0:T(8,128)S(1)} %get-tuple-element.11), channel_id=1, source_target_pairs={{0,2},{1,3},{2,0},{3,1},{4,6},{5,7},{6,4},{7,5},{8,10},{9,11},{10,... | collective-permute-start | bytes 393224 | tf_op jit(solution)/shard_map/ppermute | solution.py:119

commit v2 on v1

v2 whole, which is shorter than its diff:
```python
import functools

import jax
import jax.numpy as jnp
from jax import lax
from jax.experimental import pallas as pl
from jax.experimental.pallas import tpu as pltpu
from jax.sharding import PartitionSpec as P

VMEM = pl.BlockSpec(memory_space=pltpu.VMEM)
ANY = pl.BlockSpec(memory_space=pl.ANY)
GATES_AT_ONCE = 8
LANES = 128


def cost(flops, moved):
    return pl.CostEstimate(flops=flops, bytes_accessed=moved, transcendentals=0)


def fetch_kernel(currents_ref, green_ref, held_ref, own_ref, sems):
    copies = [
        pltpu.make_async_copy(currents_ref, held_ref, sems.at[0]),
        pltpu.make_async_copy(green_ref, own_ref, sems.at[1]),
    ]
    for copy in copies:
        copy.start()
    for copy in copies:
        copy.wait()


def fetch(currents, green):
    return pl.pallas_call(
        fetch_kernel,
        out_shape=(
            jax.ShapeDtypeStruct(currents.shape, currents.dtype),
            jax.ShapeDtypeStruct(green.shape, green.dtype),
        ),
        in_specs=[ANY, ANY],
        out_specs=(VMEM, VMEM),
        scratch_shapes=[pltpu.SemaphoreType.DMA((2,))],
        compiler_params=pltpu.CompilerParams(vmem_limit_bytes=16 << 20),
        cost_estimate=cost(0, 4 * currents.size),
        name="fetch",
    )(currents, green)


def response_kernel(offsets, chips, *refs):
    blocks = len(offsets)
    slots, currents_ref = refs[:blocks], refs[blocks]
    keep_ref, send_ref, straight_ref, crossed_ref = refs[blocks + 1 :]
    my_tx, my_cell = lax.axis_index("tx"), lax.axis_index("cell")
    my_chip, my_core = my_cell // 2, my_cell % 2
    _, freqs, cells, width = currents_ref.shape
    per_block = chips // blocks
    rows = straight_ref.shape[3]
    for f in range(freqs):
        for slot, offset in enumerate(offsets):
            block = lax.bitwise_xor(my_tx, offset)
            for j in range(per_block):
                chip = lax.bitwise_xor(block * per_block + j, my_chip)
                real = slots[slot][0, f, j * rows : (j + 1) * rows, :]
                imag = slots[slot][1, f, j * rows : (j + 1) * rows, :]
                straight_ref[f, 0, chip] = real
                straight_ref[f, 1, chip] = imag
                crossed_ref[f, 0, chip] = -imag
                crossed_ref[f, 1, chip] = real
    step = min(width, 512)
    first = my_core == 0
    for f in range(freqs):
        straight = straight_ref[f].reshape(2 * chips * rows, cells)
        crossed = crossed_ref[f].reshape(2 * chips * rows, cells)
        for at in range(0, width, step):
            cols = slice(at, at + step)
            total = jnp.dot(straight, currents_ref[0, f, :, cols], preferred_element_type=jnp.float32)
            total += jnp.dot(crossed, currents_ref[1, f, :, cols], preferred_element_type=jnp.float32)
            total = total.reshape(2, chips, 2, rows // 2, step)
            for part in range(2):
                here = 2 * f + part
                keep_ref[:, here, :, cols] = jnp.where(first, total[part, :, 0], total[part, :, 1])
                send_ref[:, here, :, cols] = jnp.where(first, total[part, :, 1], total[part, :, 0])


def responses(offsets, slots, currents, chips):
    _, freqs, block_rows, cells = slots[0].shape
    width = currents.shape[3]
    rows = block_rows * len(slots) // chips
    out = jax.ShapeDtypeStruct((chips, 2 * freqs, rows // 2, width), jnp.float32)
    products = pltpu.VMEM((freqs, 2, chips, rows, cells), jnp.bfloat16)
    return pl.pallas_call(
        functools.partial(response_kernel, offsets, chips),
        out_shape=(out, out),
        in_specs=[VMEM] * (len(slots) + 1),
        out_specs=(VMEM, VMEM),
        scratch_shapes=[products, products],
        compiler_params=pltpu.CompilerParams(vmem_limit_bytes=24 << 20),
        cost_estimate=cost(8 * freqs * chips * rows * cells * width, 4 * freqs * cells * width),
        name="responses",
    )(*slots, currents)


def gate_kernel(parts, weight_ref, *refs):
    pieces, out_ref = refs[:parts], refs[parts]
    held_ref, sems = refs[parts + 1 :]
    terms, rows, width = pieces[0].shape
    gates = out_ref.shape[0]
    blocks = [slice(at, at + LANES) for at in range(0, width, LANES)]
    total = []
    for t in range(terms):
        whole = sum(piece[t] for piece in pieces[1:]) + pieces[0][t]
        total.append([whole[:, block] for block in blocks])
    copies = []
    for at in range(0, gates, GATES_AT_ONCE):
        for g in range(at, at + GATES_AT_ONCE):
            weight = [jnp.broadcast_to(weight_ref[g, t : t + 1, :], (rows, LANES)) for t in range(terms)]
            for i, block in enumerate(blocks):
                value = weight[0] * total[0][i]
                for t in range(1, terms):
                    value += weight[t] * total[t][i]
                held_ref[g, :, block] = value
        group = pl.ds(at, GATES_AT_ONCE)
        copy = pltpu.make_async_copy(held_ref.at[group], out_ref.at[group], sems.at[at // GATES_AT_ONCE])
        copy.start()
        copies.append(copy)
    for copy in copies:
        copy.wait()


def gates_of(weights, pieces):
    gates = weights.shape[0]
    _, rows, width = pieces[0].shape
    return pl.pallas_call(
        functools.partial(gate_kernel, len(pieces)),
        out_shape=jax.ShapeDtypeStruct((gates, rows, width), jnp.float32),
        in_specs=[VMEM] * (1 + len(pieces)),
        out_specs=ANY,
        scratch_shapes=[
            pltpu.VMEM((gates, rows, width), jnp.float32),
            pltpu.SemaphoreType.DMA((gates // GATES_AT_ONCE,)),
        ],
        compiler_params=pltpu.CompilerParams(vmem_limit_bytes=24 << 20),
        name="gates",
    )(weights, *pieces)


def per_device(txs, cells, currents, green, angular_freq, gate_time):
    chips = cells // 2
    gate_phase = gate_time[:, None] * angular_freq[None, :]
    weights = jnp.stack([jnp.cos(gate_phase), -jnp.sin(gate_phase)], 2).reshape(gate_time.shape[0], -1)
    weights = jnp.broadcast_to(weights[:, :, None], weights.shape + (LANES,))

    offsets = sorted(range(1, txs), key=lambda s: (s != txs // 2, s))
    sent = [lax.ppermute(green, "tx", [(i, i ^ s) for i in range(txs)]) for s in offsets]
    held, own = fetch(currents, green)
    keep, send = responses([*offsets, 0], [*sent, own], held, chips)
    chip_sum = keep + lax.ppermute(send, "cell", [(i, i ^ 1) for i in range(cells)])
    pieces = [
        lax.ppermute(chip_sum[k], "cell", [(i, i ^ (2 * k)) for i in range(cells)]) for k in range(chips - 1, 0, -1)
    ]
    pieces.append(chip_sum[0])
    return gates_of(weights, pieces)


def solution(mesh):
    return jax.shard_map(
        functools.partial(per_device, mesh.shape["tx"], mesh.shape["cell"]),
        mesh=mesh,
        in_specs=(P(None, None, "cell", "tx"), P(None, None, "tx", "cell"), P(), P()),
        out_specs=P(None, "cell", "tx"),
        check_vma=False,
    )
```

time: 34.2 us -> 29.4 us (0.86)
  waiting for transfers between devices: 16.5 us -> 11.4 us
  local copies, waits for them, and re-layouts: 0.95 us -> 4.55 us
  Pallas kernels: 6.71 us -> 3.5 us
    ppermute x3, waiting for transfers between devices: 8.88 us -> 3.92 us  [per_device(): lax.ppermute(green, 'tx', [(i, i ^ s) for i in range(txs)])]
    unnamed x6 -> x8, local copies, waits for them, and re-layouts: 0.91 us -> 4.29 us
    pallas_call x1 -> x2, Pallas kernels: 4.69 us -> 2.04 us  [the longest x1 1.3 us: responses(): pl.pallas_call(functools.partial(response_kernel, offsets, chips), out_sh...]
    pallas_call x1, Pallas kernels: 2.02 us -> 1.46 us  [gates_of(): pl.pallas_call(functools.partial(gate_kernel, len(pieces)), out_shape=jax...]
  transfers between devices with their start and end apart: 7 -> 7, of which waited for: 6 -> 6; matrix products, arithmetic and copies ran while one was open for 1% -> 1% of each run, Pallas kernels for 0% -> 3%
where the time goes in v2:
time: 29.4 us; the launch traced here: 29 us
  waiting for transfers between devices  11.4 us (39%)
  starting transfers between devices  9.24 us (31%)
  local copies, waits for them, and re-layouts  4.55 us (15%)
  Pallas kernels  3.5 us (12%)
    ppermute x3, waiting for transfers between devices, per_device(): lax.ppermute(chip_sum[k], 'cell', [(i, i ^ 2 * k) for i in range(cells)])  5.62 us
    ppermute x3, starting transfers between devices, per_device(): lax.ppermute(green, 'tx', [(i, i ^ s) for i in range(txs)])  5.62 us
    unnamed x8, local copies, waits for them, and re-layouts  4.29 us
    ppermute x3, waiting for transfers between devices, per_device(): lax.ppermute(green, 'tx', [(i, i ^ s) for i in range(txs)])  3.92 us
    ppermute x3, starting transfers between devices, per_device(): lax.ppermute(chip_sum[k], 'cell', [(i, i ^ 2 * k) for i in range(cells)])  3.55 us
    ppermute x1, waiting for transfers between devices, per_device(): lax.ppermute(send, 'cell', [(i, i ^ 1) for i in range(cells)])  1.9 us
    pallas_call x1, Pallas kernels, gates_of(): pl.pallas_call(functools.partial(gate_kernel, len(pieces)), out_shape=jax...  1.46 us
    pallas_call x1, Pallas kernels, responses(): pl.pallas_call(functools.partial(response_kernel, offsets, chips), out_sh...  1.3 us
  transfers between devices with their start and end apart: 7, of which 6 were waited for; matrix products, arithmetic and copies ran while one was open for 1% of the time, Pallas kernels for 3%

profile of v2, /device:TPU:0, one launch (start us, length us, event | category | flops | bytes accessed | tf_op | source)
XLA Modules:
  0.0 29.0 jit_solution(3212653123510172829)
XLA Ops:
  0.0 4.0 %collective-permute-start = (bf16[2,2,16,1024]{3,2,1,0:T(8,128)(2,1)}, bf16[2,2,16,1024]{3,2,1,0:T(8,128)(2,1)S(1)}, u32[]{:S(2)}, u32[]{:S(2)}) collective-permute-start(bf16[2,2,16,1024]{3,2,1,0:T(8,128)(2,1)} %green_ref.1), channel_id=1, source_target_pairs={{0,16},{8,24},{16,0},{24,8},{1,17},{9,25},{17,1},{25,9},{2,18},{10... | collective-permute-start | bytes 393224 | tf_op jit(solution)/shard_map/ppermute | solution.py:152
  4.0 1.6 %collective-permute-start.1 = (bf16[2,2,16,1024]{3,2,1,0:T(8,128)(2,1)}, bf16[2,2,16,1024]{3,2,1,0:T(8,128)(2,1)S(1)}, u32[]{:S(2)}, u32[]{:S(2)}) collective-permute-start(bf16[2,2,16,1024]{3,2,1,0:T(8,128)(2,1)} %green_ref.1), channel_id=1, source_target_pairs={{0,8},{8,0},{16,24},{24,16},{1,9},{9,1},{17,25},{25,17},{2,10},{10... | collective-permute-start | bytes 393224 | tf_op jit(solution)/shard_map/ppermute | solution.py:152
  5.6 0.0 collective-permute-start.2
  5.6 0.0 copy-start
  5.6 3.4 %copy-done = bf16[2,2,1024,1024]{3,2,1,0:T(8,128)(2,1)S(1)} copy-done((bf16[2,2,1024,1024]{3,2,1,0:T(8,128)(2,1)S(1)}, bf16[2,2,1024,1024]{3,2,1,0:T(8,128)(2,1)}, u32[]{:S(2)}) %copy-start) | copy-done | bytes 8388632
  9.0 0.0 copy-start.1
  9.0 0.9 %copy-done.1 = bf16[2,2,16,1024]{3,2,1,0:T(8,128)(2,1)S(1)} copy-done((bf16[2,2,16,1024]{3,2,1,0:T(8,128)(2,1)S(1)}, bf16[2,2,16,1024]{3,2,1,0:T(8,128)(2,1)}, u32[]{:S(2)}) %copy-start.1) | copy-done | bytes 131096
  9.9 0.0 copy-start.2
  9.9 0.0 copy-start.3
  9.9 0.7 %fetch.1 = (bf16[2,2,1024,1024]{3,2,1,0:T(8,128)(2,1)S(1)}, bf16[2,2,16,1024]{3,2,1,0:T(8,128)(2,1)S(1)}) custom-call(bf16[2,2,1024,1024]{3,2,1,0:T(8,128)(2,1)S(1)} %copy-done, bf16[2,2,16,1024]{3,2,1,0:T(8,128)(2,1)S(1)} %copy-done.1), custom_call_target="tpu_custom_call" | custom-call | bytes 16777216 | tf_op jit(solution)/shard_map/fetch/pallas_call | solution.py:32
  10.7 1.5 %collective-permute-done.refs_0_ = bf16[2,2,16,1024]{3,2,1,0:T(8,128)(2,1)S(1)} collective-permute-done((bf16[2,2,16,1024]{3,2,1,0:T(8,128)(2,1)}, bf16[2,2,16,1024]{3,2,1,0:T(8,128)(2,1)S(1)}, u32[]{:S(2)}, u32[]{:S(2)}) %collective-permute-start) | collective-permute-done | bytes 131104 | tf_op jit(solution)/shard_map/ppermute | solution.py:152
  12.2 0.0 collective-permute-done.1.refs_1_
  12.2 2.4 %collective-permute-done.2.refs_2_ = bf16[2,2,16,1024]{3,2,1,0:T(8,128)(2,1)S(1)} collective-permute-done((bf16[2,2,16,1024]{3,2,1,0:T(8,128)(2,1)}, bf16[2,2,16,1024]{3,2,1,0:T(8,128)(2,1)S(1)}, u32[]{:S(2)}, u32[]{:S(2)}) %collective-permute-start.2) | collective-permute-done | bytes 131104 | tf_op jit(solution)/shard_map/ppermute | solution.py:152
  14.6 1.3 %responses.1 = (f32[4,4,8,1024]{3,2,1,0:T(8,128)S(1)}, f32[4,4,8,1024]{3,2,1,0:T(8,128)S(1)}) custom-call(bf16[2,2,16,1024]{3,2,1,0:T(8,128)(2,1)S(1)} %collective-permute-done.refs_0_, bf16[2,2,16,1024]{3,2,1,0:T(8,128)(2,1)S(1)} %collective-permute-done.1.refs_1_, bf16[2,2,16,1024]{3,2,1,0:T(8,128)(2,1)S(1)} %collective-permute-done.2.refs_2_, ...), custom_call_target="tpu_custom_call" | custom-call | flops 1073741824 | bytes 8388608 | tf_op jit(solution)/shard_map/responses/pallas_call | solution.py:89
  15.9 0.1 collective-permute-start.3
  16.0 1.9 %collective-permute-done.3 = f32[4,4,8,1024]{3,2,1,0:T(8,128)S(1)} collective-permute-done((f32[4,4,8,1024]{3,2,1,0:T(8,128)S(1)}, f32[4,4,8,1024]{3,2,1,0:T(8,128)S(1)}, u32[]{:S(2)}, u32[]{:S(2)}) %collective-permute-start.3) | collective-permute-done | bytes 524320 | tf_op jit(solution)/shard_map/ppermute | solution.py:155
  17.9 0.1 add.3
  18.0 2.5 %collective-permute-start.4 = (f32[4,8,1024]{2,1,0:T(8,128)S(1)}, f32[4,8,1024]{2,1,0:T(8,128)S(1)}, u32[]{:S(2)}, u32[]{:S(2)}) collective-permute-start(f32[4,8,1024]{2,1,0:T(8,128)S(1)} %get-tuple-element.16), channel_id=1, source_target_pairs={{0,6},{1,7},{2,4},{3,5},{4,2},{5,3},{6,0},{7,1},{8,14},{9,15},{10,... | collective-permute-start | bytes 393224 | tf_op jit(solution)/shard_map/ppermute | solution.py:157
  20.5 0.5 %collective-permute-start.5 = (f32[4,8,1024]{2,1,0:T(8,128)S(1)}, f32[4,8,1024]{2,1,0:T(8,128)S(1)}, u32[]{:S(2)}, u32[]{:S(2)}) collective-permute-start(f32[4,8,1024]{2,1,0:T(8,128)S(1)} %get-tuple-element.15), channel_id=1, source_target_pairs={{0,4},{1,5},{2,6},{3,7},{4,0},{5,1},{6,2},{7,3},{8,12},{9,13},{10,... | collective-permute-start | bytes 393224 | tf_op jit(solution)/shard_map/ppermute | solution.py:157
  21.0 0.5 %collective-permute-start.6 = (f32[4,8,1024]{2,1,0:T(8,128)S(1)}, f32[4,8,1024]{2,1,0:T(8,128)S(1)}, u32[]{:S(2)}, u32[]{:S(2)}) collective-permute-start(f32[4,8,1024]{2,1,0:T(8,128)S(1)} %get-tuple-element.14), channel_id=1, source_target_pairs={{0,2},{1,3},{2,0},{3,1},{4,6},{5,7},{6,4},{7,5},{8,10},{9,11},{10,... | collective-permute-start | bytes 393224 | tf_op jit(solution)/shard_map/ppermute | solution.py:157
  21.5 0.0 copy-done.2
  21.5 0.0 copy-done.3
  21.5 0.1 multiply_cosine_fusion
  21.7 0.1 copy.7
  21.8 3.0 %collective-permute-done.4.refs_0_ = f32[4,8,1024]{2,1,0:T(8,128)S(1)} collective-permute-done((f32[4,8,1024]{2,1,0:T(8,128)S(1)}, f32[4,8,1024]{2,1,0:T(8,128)S(1)}, u32[]{:S(2)}, u32[]{:S(2)}) %collective-permute-start.4) | collective-permute-done | bytes 131104 | tf_op jit(solution)/shard_map/ppermute | solution.py:157
  24.8 2.5 %collective-permute-done.5.refs_1_ = f32[4,8,1024]{2,1,0:T(8,128)S(1)} collective-permute-done((f32[4,8,1024]{2,1,0:T(8,128)S(1)}, f32[4,8,1024]{2,1,0:T(8,128)S(1)}, u32[]{:S(2)}, u32[]{:S(2)}) %collective-permute-start.5) | collective-permute-done | bytes 131104 | tf_op jit(solution)/shard_map/ppermute | solution.py:157
  27.3 0.1 collective-permute-done.6.refs_2_
  27.4 0.1 broadcast_in_dim.10.weight_ref
  27.5 1.5 %gates.1 = f32[64,8,1024]{2,1,0:T(8,128)} custom-call(f32[64,4,128]{2,1,0:T(4,128)S(1)} %broadcast_in_dim.10.weight_ref, f32[4,8,1024]{2,1,0:T(8,128)S(1)} %collective-permute-done.4.refs_0_, f32[4,8,1024]{2,1,0:T(8,128)S(1)} %collective-permute-done.5.refs_1_, f32[4,8,1024]{2,1,0:T(8,128)S(1)} %collective-permute-done.6.refs_2_, ...), custom_call_target="tpu_custom_call" | custom-call | tf_op jit(solution)/shard_map/gates/pallas_call | solution.py:131
  (3 shorter events, 0.0 us)
Async XLA Ops:
  0.0 12.2 %collective-permute-start = (bf16[2,2,16,1024]{3,2,1,0:T(8,128)(2,1)}, bf16[2,2,16,1024]{3,2,1,0:T(8,128)(2,1)S(1)}, u32[]{:S(2)}, u32[]{:S(2)}) collective-permute-start(bf16[2,2,16,1024]{3,2,1,0:T(8,128)(2,1)} %green_ref.1), channel_id=1, source_target_pairs={{0,16},{8,24},{16,0},{24,8},{1,17},{9,25},{17,1},{25,9},{2,18},{10... | collective-permute-start | bytes 393224 | tf_op jit(solution)/shard_map/ppermute | solution.py:152
  4.0 8.2 %collective-permute-start.1 = (bf16[2,2,16,1024]{3,2,1,0:T(8,128)(2,1)}, bf16[2,2,16,1024]{3,2,1,0:T(8,128)(2,1)S(1)}, u32[]{:S(2)}, u32[]{:S(2)}) collective-permute-start(bf16[2,2,16,1024]{3,2,1,0:T(8,128)(2,1)} %green_ref.1), channel_id=1, source_target_pairs={{0,8},{8,0},{16,24},{24,16},{1,9},{9,1},{17,25},{25,17},{2,10},{10... | collective-permute-start | bytes 393224 | tf_op jit(solution)/shard_map/ppermute | solution.py:152
  5.6 9.0 %collective-permute-start.2 = (bf16[2,2,16,1024]{3,2,1,0:T(8,128)(2,1)}, bf16[2,2,16,1024]{3,2,1,0:T(8,128)(2,1)S(1)}, u32[]{:S(2)}, u32[]{:S(2)}) collective-permute-start(bf16[2,2,16,1024]{3,2,1,0:T(8,128)(2,1)} %green_ref.1), channel_id=1, source_target_pairs={{0,24},{8,16},{16,8},{24,0},{1,25},{9,17},{17,9},{25,1},{2,26},{10... | collective-permute-start | bytes 393224 | tf_op jit(solution)/shard_map/ppermute | solution.py:152
  5.6 3.4 %copy-start = (bf16[2,2,1024,1024]{3,2,1,0:T(8,128)(2,1)S(1)}, bf16[2,2,1024,1024]{3,2,1,0:T(8,128)(2,1)}, u32[]{:S(2)}) copy-start(bf16[2,2,1024,1024]{3,2,1,0:T(8,128)(2,1)} %currents_ref.1) | copy-start | bytes 25165828
  9.0 0.9 %copy-start.1 = (bf16[2,2,16,1024]{3,2,1,0:T(8,128)(2,1)S(1)}, bf16[2,2,16,1024]{3,2,1,0:T(8,128)(2,1)}, u32[]{:S(2)}) copy-start(bf16[2,2,16,1024]{3,2,1,0:T(8,128)(2,1)} %green_ref.1) | copy-start | bytes 393220
  9.9 11.6 %copy-start.2 = (f32[64]{0:T(128)S(1)}, f32[64]{0:T(128)}, u32[]{:S(2)}) copy-start(f32[64]{0:T(128)} %param.7) | copy-start | bytes 772
  9.9 11.6 %copy-start.3 = (f32[2]{0:T(128)S(1)}, f32[2]{0:T(128)}, u32[]{:S(2)}) copy-start(f32[2]{0:T(128)} %param.6) | copy-start | bytes 28
  15.9 2.0 %collective-permute-start.3 = (f32[4,4,8,1024]{3,2,1,0:T(8,128)S(1)}, f32[4,4,8,1024]{3,2,1,0:T(8,128)S(1)}, u32[]{:S(2)}, u32[]{:S(2)}) collective-permute-start(f32[4,4,8,1024]{3,2,1,0:T(8,128)S(1)} %get-tuple-element.12), channel_id=1, source_target_pairs={{0,1},{1,0},{2,3},{3,2},{4,5},{5,4},{6,7},{7,6},{8,9},{9,8},{10,11... | collective-permute-start | bytes 1572872 | tf_op jit(solution)/shard_map/ppermute | solution.py:155
  18.0 6.8 %collective-permute-start.4 = (f32[4,8,1024]{2,1,0:T(8,128)S(1)}, f32[4,8,1024]{2,1,0:T(8,128)S(1)}, u32[]{:S(2)}, u32[]{:S(2)}) collective-permute-start(f32[4,8,1024]{2,1,0:T(8,128)S(1)} %get-tuple-element.16), channel_id=1, source_target_pairs={{0,6},{1,7},{2,4},{3,5},{4,2},{5,3},{6,0},{7,1},{8,14},{9,15},{10,... | collective-permute-start | bytes 393224 | tf_op jit(solution)/shard_map/ppermute | solution.py:157
  20.5 6.8 %collective-permute-start.5 = (f32[4,8,1024]{2,1,0:T(8,128)S(1)}, f32[4,8,1024]{2,1,0:T(8,128)S(1)}, u32[]{:S(2)}, u32[]{:S(2)}) collective-permute-start(f32[4,8,1024]{2,1,0:T(8,128)S(1)} %get-tuple-element.15), channel_id=1, source_target_pairs={{0,4},{1,5},{2,6},{3,7},{4,0},{5,1},{6,2},{7,3},{8,12},{9,13},{10,... | collective-permute-start | bytes 393224 | tf_op jit(solution)/shard_map/ppermute | solution.py:157
  21.0 6.4 %collective-permute-start.6 = (f32[4,8,1024]{2,1,0:T(8,128)S(1)}, f32[4,8,1024]{2,1,0:T(8,128)S(1)}, u32[]{:S(2)}, u32[]{:S(2)}) collective-permute-start(f32[4,8,1024]{2,1,0:T(8,128)S(1)} %get-tuple-element.14), channel_id=1, source_target_pairs={{0,2},{1,3},{2,0},{3,1},{4,6},{5,7},{6,4},{7,5},{8,10},{9,11},{10,... | collective-permute-start | bytes 393224 | tf_op jit(solution)/shard_map/ppermute | solution.py:157

commit v3 on v2

v3 whole, which is shorter than its diff:
```python
import functools

import jax
import jax.numpy as jnp
from jax import lax
from jax.experimental import pallas as pl
from jax.experimental.pallas import tpu as pltpu
from jax.sharding import PartitionSpec as P

VMEM = pl.BlockSpec(memory_space=pltpu.VMEM)
ANY = pl.BlockSpec(memory_space=pl.ANY)
GATES_AT_ONCE = 8
LANES = 128


def cost(flops, moved):
    return pl.CostEstimate(flops=flops, bytes_accessed=moved, transcendentals=0)


def response_kernel(freq, offsets, chips, *refs):
    blocks = len(offsets)
    slots, currents_ref = refs[:blocks], refs[blocks]
    keep_ref, send_ref, straight_ref, crossed_ref = refs[blocks + 1 :]
    my_tx, my_cell = lax.axis_index("tx"), lax.axis_index("cell")
    my_chip, my_core = my_cell // 2, my_cell % 2
    _, _, cells, width = currents_ref.shape
    per_block = chips // blocks
    rows = straight_ref.shape[2]
    for slot, offset in enumerate(offsets):
        block = lax.bitwise_xor(my_tx, offset)
        whole = len(slots[slot].shape) == 4
        for j in range(per_block):
            chip = lax.bitwise_xor(block * per_block + j, my_chip)
            here = slice(j * rows, (j + 1) * rows)
            real = slots[slot][0, freq, here, :] if whole else slots[slot][0, here, :]
            imag = slots[slot][1, freq, here, :] if whole else slots[slot][1, here, :]
            straight_ref[0, chip] = real
            straight_ref[1, chip] = imag
            crossed_ref[0, chip] = -imag
            crossed_ref[1, chip] = real
    step = min(width, 512)
    first = my_core == 0
    straight = straight_ref[...].reshape(2 * chips * rows, cells)
    crossed = crossed_ref[...].reshape(2 * chips * rows, cells)
    for at in range(0, width, step):
        cols = slice(at, at + step)
        total = jnp.dot(straight, currents_ref[0, freq, :, cols], preferred_element_type=jnp.float32)
        total += jnp.dot(crossed, currents_ref[1, freq, :, cols], preferred_element_type=jnp.float32)
        total = total.reshape(2, chips, 2, rows // 2, step)
        for part in range(2):
            keep_ref[:, part, :, cols] = jnp.where(first, total[part, :, 0], total[part, :, 1])
            send_ref[:, part, :, cols] = jnp.where(first, total[part, :, 1], total[part, :, 0])


def responses(freq, offsets, slots, currents, chips):
    _, _, cells, width = currents.shape
    rows = slots[0].shape[-2] * len(slots) // chips
    out = jax.ShapeDtypeStruct((chips, 2, rows // 2, width), jnp.float32)
    products = pltpu.VMEM((2, chips, rows, cells), jnp.bfloat16)
    return pl.pallas_call(
        functools.partial(response_kernel, freq, offsets, chips),
        out_shape=(out, out),
        in_specs=[VMEM] * (len(slots) + 1),
        out_specs=(VMEM, VMEM),
        scratch_shapes=[products, products],
        compiler_params=pltpu.CompilerParams(vmem_limit_bytes=16 << 20),
        cost_estimate=cost(8 * chips * rows * cells * width, 4 * cells * width),
        name="responses",
    )(*slots, currents)


def gate_kernel(parts, weight_ref, *refs):
    pieces, out_ref = refs[:parts], refs[parts]
    held_ref, sems = refs[parts + 1 :]
    terms, rows, width = pieces[0].shape
    gates = out_ref.shape[0]
    blocks = [slice(at, at + LANES) for at in range(0, width, LANES)]
    total = []
    for t in range(terms):
        whole = sum(piece[t] for piece in pieces[1:]) + pieces[0][t]
        total.append([whole[:, block] for block in blocks])
    copies = []
    for at in range(0, gates, GATES_AT_ONCE):
        for g in range(at, at + GATES_AT_ONCE):
            weight = [jnp.broadcast_to(weight_ref[g, t : t + 1, :], (rows, LANES)) for t in range(terms)]
            for i, block in enumerate(blocks):
                value = weight[0] * total[0][i]
                for t in range(1, terms):
                    value += weight[t] * total[t][i]
                held_ref[g, :, block] = value
        group = pl.ds(at, GATES_AT_ONCE)
        copy = pltpu.make_async_copy(held_ref.at[group], out_ref.at[group], sems.at[at // GATES_AT_ONCE])
        copy.start()
        copies.append(copy)
    for copy in copies:
        copy.wait()


def gates_of(weights, pieces):
    gates = weights.shape[0]
    _, rows, width = pieces[0].shape
    return pl.pallas_call(
        functools.partial(gate_kernel, len(pieces)),
        out_shape=jax.ShapeDtypeStruct((gates, rows, width), jnp.float32),
        in_specs=[VMEM] * (1 + len(pieces)),
        out_specs=ANY,
        scratch_shapes=[
            pltpu.VMEM((gates, rows, width), jnp.float32),
            pltpu.SemaphoreType.DMA((gates // GATES_AT_ONCE,)),
        ],
        compiler_params=pltpu.CompilerParams(vmem_limit_bytes=24 << 20),
        name="gates",
    )(weights, *pieces)


def lane_kernel(weight_ref, out_ref):
    out_ref[...] = jnp.broadcast_to(weight_ref[...][:, :, None], out_ref.shape)


def lane_copies(weights):
    return pl.pallas_call(
        lane_kernel,
        out_shape=jax.ShapeDtypeStruct(weights.shape + (LANES,), weights.dtype),
        in_specs=[VMEM],
        out_specs=VMEM,
        compiler_params=pltpu.CompilerParams(vmem_limit_bytes=8 << 20),
        cost_estimate=cost(4 << 30, 1 << 20),
        name="weights",
    )(weights)


def per_device(txs, cells, currents, green, angular_freq, gate_time):
    chips = cells // 2
    gate_phase = gate_time[:, None] * angular_freq[None, :]
    weights = lane_copies(jnp.stack([jnp.cos(gate_phase), -jnp.sin(gate_phase)], 2).reshape(gate_time.shape[0], -1))

    def swap(a, axis, bit):
        return lax.ppermute(a, axis, [(i, i ^ bit) for i in range({"tx": txs, "cell": cells}[axis])])

    freqs = currents.shape[1]
    own = [green[:, f] for f in range(freqs)]
    far = [swap(own[f], "tx", txs // 2) for f in range(freqs)]
    near = swap(lax.optimization_barrier((green, own[-1]))[0], "tx", 1)
    far[0], weights = lax.optimization_barrier((far[0], weights))
    keeps, gots = [], []
    for f in range(freqs):
        slots = {0: own[f], 1: near, txs // 2: far[f], txs // 2 + 1: swap(far[f], "tx", 1)}
        offsets = [txs // 2, 1, txs // 2 + 1, 0]
        keep, send = responses(f, offsets, [slots[s] for s in offsets], currents, chips)
        keeps.append(keep)
        gots.append(swap(send, "cell", 1))
    sums = jnp.concatenate([keep + got for keep, got in zip(keeps, gots)], 1)
    pieces = [swap(sums[k], "cell", 2 * k) for k in range(chips - 1, 0, -1)] + [sums[0]]
    return gates_of(weights, pieces)


def solution(mesh):
    return jax.shard_map(
        functools.partial(per_device, mesh.shape["tx"], mesh.shape["cell"]),
        mesh=mesh,
        in_specs=(P(None, None, "cell", "tx"), P(None, None, "tx", "cell"), P(), P()),
        out_specs=P(None, "cell", "tx"),
        check_vma=False,
    )
```

time: 29.4 us -> 29.1 us (0.990)
  starting transfers between devices: 9.24 us -> 13.1 us
  local copies, waits for them, and re-layouts: 4.55 us -> 0.98 us
  other arithmetic: 0.2 us -> 0.9 us
  waiting for transfers between devices: 11.4 us -> 10.9 us
  Pallas kernels: 3.5 us -> 3.02 us
    unnamed x8 -> x2, local copies, waits for them, and re-layouts: 4.29 us -> 0.01 us
    ppermute x7 -> x10, starting transfers between devices: 9.24 us -> 13.1 us  [swap(): lax.ppermute(a, axis, [(i, i ^ bit) for i in range({'tx': txs, 'cell': ce...]
    squeeze x1, local copies, waits for them, and re-layouts: 0.04 us -> 0.88 us  [per_device(): own = [green[:, f] for f in range(freqs)]]
    cos x1, other arithmetic: 0.11 us -> 0.78 us  [per_device(): jnp.cos(gate_phase)]
    ppermute x7 -> x10, waiting for transfers between devices: 11.4 us -> 10.9 us  [swap(): lax.ppermute(a, axis, [(i, i ^ bit) for i in range({'tx': txs, 'cell': ce...]
    pallas_call x2 -> x3, Pallas kernels: 2.04 us -> 1.57 us  [the longest x2 1.45 us: responses(): pl.pallas_call(functools.partial(response_kernel, freq, offsets, chips),...]
  transfers between devices with their start and end apart: 7 -> 10, of which waited for: 6 -> 9; matrix products, arithmetic and copies ran while one was open for 1% -> 3% of each run, Pallas kernels for 3% -> 5%
where the time goes in v3:
time: 29.1 us; the launch traced here: 28.9 us
  starting transfers between devices  13.1 us (45%)
  waiting for transfers between devices  10.9 us (37%)
  Pallas kernels  3.02 us (10%)
  local copies, waits for them, and re-layouts  0.98 us (3%)
  other arithmetic  0.9 us (3%)
    ppermute x10, starting transfers between devices, swap(): lax.ppermute(a, axis, [(i, i ^ bit) for i in range({'tx': txs, 'cell': ce...  13.1 us
    ppermute x10, waiting for transfers between devices, swap(): lax.ppermute(a, axis, [(i, i ^ bit) for i in range({'tx': txs, 'cell': ce...  10.9 us
    pallas_call x1, Pallas kernels, gates_of(): pl.pallas_call(functools.partial(gate_kernel, len(pieces)), out_shape=jax...  1.45 us
    pallas_call x2, Pallas kernels, responses(): pl.pallas_call(functools.partial(response_kernel, freq, offsets, chips),...  1.45 us
    squeeze x1, local copies, waits for them, and re-layouts, per_device(): own = [green[:, f] for f in range(freqs)]  0.88 us
    cos x1, other arithmetic, per_device(): jnp.cos(gate_phase)  0.78 us
  transfers between devices with their start and end apart: 10, of which 9 were waited for; matrix products, arithmetic and copies ran while one was open for 3% of the time, Pallas kernels for 5%

profile of v3, /device:TPU:0, one launch (start us, length us, event | category | flops | bytes accessed | tf_op | source)
XLA Modules:
  0.0 28.9 jit_solution(7693919486717084093)
XLA Ops:
  0.0 0.9 %slice_bitcast_fusion = (bf16[2,16,1024]{2,1,0:T(8,128)(2,1)S(1)}, bf16[2,16,1024]{2,1,0:T(8,128)(2,1)S(1)}) fusion(bf16[2,2,16,1024]{3,2,1,0:T(8,128)(2,1)} %param.5), kind=kLoop, calls=%fused_computation.14 | loop fusion | bytes 262144 | tf_op jit(solution)/shard_map/squeeze | solution.py:141
  0.9 4.1 %collective-permute-start = (bf16[2,16,1024]{2,1,0:T(8,128)(2,1)S(1)}, bf16[2,16,1024]{2,1,0:T(8,128)(2,1)S(1)}, u32[]{:S(2)}, u32[]{:S(2)}) collective-permute-start(bf16[2,16,1024]{2,1,0:T(8,128)(2,1)S(1)} %get-tuple-element.24.refs_3_), channel_id=1, source_target_pairs={{0,16},{8,24},{16,0},{24,8},{1,17},{9,25},{17,1},{25,9},{2,18},{10... | collective-permute-start | bytes 196616 | tf_op jit(solution)/shard_map/ppermute | solution.py:138
  5.0 0.1 collective-permute-start.4
  5.1 1.8 %collective-permute-start.1 = (bf16[2,2,16,1024]{3,2,1,0:T(8,128)(2,1)}, bf16[2,2,16,1024]{3,2,1,0:T(8,128)(2,1)S(1)}, u32[]{:S(2)}, u32[]{:S(2)}) collective-permute-start(bf16[2,2,16,1024]{3,2,1,0:T(8,128)(2,1)} %param.5), channel_id=1, source_target_pairs={{0,8},{8,0},{16,24},{24,16},{1,9},{9,1},{17,25},{25,17},{2,10},{10... | collective-permute-start | bytes 393224 | tf_op jit(solution)/shard_map/ppermute | solution.py:138
  6.9 0.8 %multiply_cosine_fusion = (f32[64,2,1]{0,1,2:T(2,128)S(1)}, f32[64,2,1]{0,1,2:T(2,128)S(1)}) fusion(f32[64]{0:T(128)} %param.7, f32[2]{0:T(128)} %param.6), kind=kLoop, calls=%fused_computation.18 | loop fusion | flops 256 | bytes 1288 | tf_op jit(solution)/shard_map/cos | solution.py:135
  7.7 0.1 copy.12.weight_ref
  7.8 0.0 copy-start
  7.8 0.1 weights.1.weight_ref
  7.9 0.8 %collective-permute-done.refs_0_ = bf16[2,16,1024]{2,1,0:T(8,128)(2,1)S(1)} collective-permute-done((bf16[2,16,1024]{2,1,0:T(8,128)(2,1)S(1)}, bf16[2,16,1024]{2,1,0:T(8,128)(2,1)S(1)}, u32[]{:S(2)}, u32[]{:S(2)}) %collective-permute-start) | collective-permute-done | bytes 65568 | tf_op jit(solution)/shard_map/ppermute | solution.py:138
  8.7 1.9 %collective-permute-start.2 = (bf16[2,16,1024]{2,1,0:T(8,128)(2,1)S(1)}, bf16[2,16,1024]{2,1,0:T(8,128)(2,1)S(1)}, u32[]{:S(2)}, u32[]{:S(2)}) collective-permute-start(bf16[2,16,1024]{2,1,0:T(8,128)(2,1)S(1)} %collective-permute-done.refs_0_), channel_id=1, source_target_pairs={{0,8},{8,0},{16,24},{24,16},{1,9},{9,1},{17,25},{25,17},{2,10},{10... | collective-permute-start | bytes 196616 | tf_op jit(solution)/shard_map/ppermute | solution.py:138
  10.6 0.3 %collective-permute-done.4.refs_0_ = bf16[2,16,1024]{2,1,0:T(8,128)(2,1)S(1)} collective-permute-done((bf16[2,16,1024]{2,1,0:T(8,128)(2,1)S(1)}, bf16[2,16,1024]{2,1,0:T(8,128)(2,1)S(1)}, u32[]{:S(2)}, u32[]{:S(2)}) %collective-permute-start.4) | collective-permute-done | bytes 65568 | tf_op jit(solution)/shard_map/ppermute | solution.py:138
  11.0 1.5 %collective-permute-start.5 = (bf16[2,16,1024]{2,1,0:T(8,128)(2,1)S(1)}, bf16[2,16,1024]{2,1,0:T(8,128)(2,1)S(1)}, u32[]{:S(2)}, u32[]{:S(2)}) collective-permute-start(bf16[2,16,1024]{2,1,0:T(8,128)(2,1)S(1)} %collective-permute-done.4.refs_0_), channel_id=1, source_target_pairs={{0,8},{8,0},{16,24},{24,16},{1,9},{9,1},{17,25},{25,17},{2,10},{10... | collective-permute-start | bytes 196616 | tf_op jit(solution)/shard_map/ppermute | solution.py:138
  12.4 1.5 %collective-permute-done.2.refs_2_ = bf16[2,16,1024]{2,1,0:T(8,128)(2,1)S(1)} collective-permute-done((bf16[2,16,1024]{2,1,0:T(8,128)(2,1)S(1)}, bf16[2,16,1024]{2,1,0:T(8,128)(2,1)S(1)}, u32[]{:S(2)}, u32[]{:S(2)}) %collective-permute-start.2) | collective-permute-done | bytes 65568 | tf_op jit(solution)/shard_map/ppermute | solution.py:138
  13.9 0.0 collective-permute-done.1.refs_1_
  13.9 0.0 copy-done
  13.9 0.7 %responses.2 = (f32[4,2,8,1024]{3,2,1,0:T(8,128)S(1)}, f32[4,2,8,1024]{3,2,1,0:T(8,128)S(1)}) custom-call(bf16[2,16,1024]{2,1,0:T(8,128)(2,1)S(1)} %collective-permute-done.refs_0_, bf16[2,2,16,1024]{3,2,1,0:T(8,128)(2,1)S(1)} %collective-permute-done.1.refs_1_, bf16[2,16,1024]{2,1,0:T(8,128)(2,1)S(1)} %collective-permute-done.2.refs_2_, ...), custom_call_target="tpu_custom_call" | custom-call | flops 536870912 | bytes 4194304 | tf_op jit(solution)/shard_map/responses/pallas_call | solution.py:60
  14.6 0.1 collective-permute-start.3
  14.7 0.5 %collective-permute-done.5.refs_2_ = bf16[2,16,1024]{2,1,0:T(8,128)(2,1)S(1)} collective-permute-done((bf16[2,16,1024]{2,1,0:T(8,128)(2,1)S(1)}, bf16[2,16,1024]{2,1,0:T(8,128)(2,1)S(1)}, u32[]{:S(2)}, u32[]{:S(2)}) %collective-permute-start.5) | collective-permute-done | bytes 65568 | tf_op jit(solution)/shard_map/ppermute | solution.py:138
  15.2 0.7 %responses.3 = (f32[4,2,8,1024]{3,2,1,0:T(8,128)S(1)}, f32[4,2,8,1024]{3,2,1,0:T(8,128)S(1)}) custom-call(bf16[2,16,1024]{2,1,0:T(8,128)(2,1)S(1)} %collective-permute-done.4.refs_0_, bf16[2,2,16,1024]{3,2,1,0:T(8,128)(2,1)S(1)} %collective-permute-done.1.refs_1_, bf16[2,16,1024]{2,1,0:T(8,128)(2,1)S(1)} %collective-permute-done.5.refs_2_, ...), custom_call_target="tpu_custom_call" | custom-call | flops 536870912 | bytes 4194304 | tf_op jit(solution)/shard_map/responses/pallas_call | solution.py:60
  16.0 0.1 collective-permute-start.6
  16.0 0.2 collective-permute-done.3
  16.3 1.3 %collective-permute-done.6 = f32[4,2,8,1024]{3,2,1,0:T(8,128)S(1)} collective-permute-done((f32[4,2,8,1024]{3,2,1,0:T(8,128)S(1)}, f32[4,2,8,1024]{3,2,1,0:T(8,128)S(1)}, u32[]{:S(2)}, u32[]{:S(2)}) %collective-permute-start.6) | collective-permute-done | bytes 262176 | tf_op jit(solution)/shard_map/ppermute | solution.py:138
  17.7 2.9 %collective-permute-start.7 = (f32[4,8,1024]{2,1,0:T(8,128)S(1)}, f32[4,8,1024]{2,1,0:T(8,128)S(1)}, u32[]{:S(2)}, u32[]{:S(2)}) collective-permute-start(f32[4,8,1024]{2,1,0:T(8,128)S(1)} %get-tuple-element.20), channel_id=1, source_target_pairs={{0,6},{1,7},{2,4},{3,5},{4,2},{5,3},{6,0},{7,1},{8,14},{9,15},{10,... | collective-permute-start | bytes 393224 | tf_op jit(solution)/shard_map/ppermute | solution.py:138
  20.6 0.5 %collective-permute-start.8 = (f32[4,8,1024]{2,1,0:T(8,128)S(1)}, f32[4,8,1024]{2,1,0:T(8,128)S(1)}, u32[]{:S(2)}, u32[]{:S(2)}) collective-permute-start(f32[4,8,1024]{2,1,0:T(8,128)S(1)} %get-tuple-element.21), channel_id=1, source_target_pairs={{0,4},{1,5},{2,6},{3,7},{4,0},{5,1},{6,2},{7,3},{8,12},{9,13},{10,... | collective-permute-start | bytes 393224 | tf_op jit(solution)/shard_map/ppermute | solution.py:138
  21.1 0.1 collective-permute-start.9
  21.2 3.3 %collective-permute-done.7.refs_0_ = f32[4,8,1024]{2,1,0:T(8,128)S(1)} collective-permute-done((f32[4,8,1024]{2,1,0:T(8,128)S(1)}, f32[4,8,1024]{2,1,0:T(8,128)S(1)}, u32[]{:S(2)}, u32[]{:S(2)}) %collective-permute-start.7) | collective-permute-done | bytes 131104 | tf_op jit(solution)/shard_map/ppermute | solution.py:138
  24.5 2.7 %collective-permute-done.8.refs_1_ = f32[4,8,1024]{2,1,0:T(8,128)S(1)} collective-permute-done((f32[4,8,1024]{2,1,0:T(8,128)S(1)}, f32[4,8,1024]{2,1,0:T(8,128)S(1)}, u32[]{:S(2)}, u32[]{:S(2)}) %collective-permute-start.8) | collective-permute-done | bytes 131104 | tf_op jit(solution)/shard_map/ppermute | solution.py:138
  27.2 0.3 collective-permute-done.9.refs_2_
  27.5 1.5 %gates.1 = f32[64,8,1024]{2,1,0:T(8,128)} custom-call(f32[64,4,128]{2,1,0:T(4,128)S(1)} %weights.1.weight_ref, f32[4,8,1024]{2,1,0:T(8,128)S(1)} %collective-permute-done.7.refs_0_, f32[4,8,1024]{2,1,0:T(8,128)S(1)} %collective-permute-done.8.refs_1_, f32[4,8,1024]{2,1,0:T(8,128)S(1)} %collective-permute-done.9.refs_2_, ...), custom_call_target="tpu_custom_call" | custom-call | tf_op jit(solution)/shard_map/gates/pallas_call | solution.py:102
  (5 shorter events, 0.1 us)
Async XLA Ops:
  0.9 7.9 %collective-permute-start = (bf16[2,16,1024]{2,1,0:T(8,128)(2,1)S(1)}, bf16[2,16,1024]{2,1,0:T(8,128)(2,1)S(1)}, u32[]{:S(2)}, u32[]{:S(2)}) collective-permute-start(bf16[2,16,1024]{2,1,0:T(8,128)(2,1)S(1)} %get-tuple-element.24.refs_3_), channel_id=1, source_target_pairs={{0,16},{8,24},{16,0},{24,8},{1,17},{9,25},{17,1},{25,9},{2,18},{10... | collective-permute-start | bytes 196616 | tf_op jit(solution)/shard_map/ppermute | solution.py:138
  5.0 6.0 %collective-permute-start.4 = (bf16[2,16,1024]{2,1,0:T(8,128)(2,1)S(1)}, bf16[2,16,1024]{2,1,0:T(8,128)(2,1)S(1)}, u32[]{:S(2)}, u32[]{:S(2)}) collective-permute-start(bf16[2,16,1024]{2,1,0:T(8,128)(2,1)S(1)} %get-tuple-element.23.refs_3_), channel_id=1, source_target_pairs={{0,16},{8,24},{16,0},{24,8},{1,17},{9,25},{17,1},{25,9},{2,18},{10... | collective-permute-start | bytes 196616 | tf_op jit(solution)/shard_map/ppermute | solution.py:138
  5.1 8.8 %collective-permute-start.1 = (bf16[2,2,16,1024]{3,2,1,0:T(8,128)(2,1)}, bf16[2,2,16,1024]{3,2,1,0:T(8,128)(2,1)S(1)}, u32[]{:S(2)}, u32[]{:S(2)}) collective-permute-start(bf16[2,2,16,1024]{3,2,1,0:T(8,128)(2,1)} %param.5), channel_id=1, source_target_pairs={{0,8},{8,0},{16,24},{24,16},{1,9},{9,1},{17,25},{25,17},{2,10},{10... | collective-permute-start | bytes 393224 | tf_op jit(solution)/shard_map/ppermute | solution.py:138
  7.8 6.1 %copy-start = (bf16[2,2,1024,1024]{3,2,1,0:T(8,128)(2,1)S(1)}, bf16[2,2,1024,1024]{3,2,1,0:T(8,128)(2,1)}, u32[]{:S(2)}) copy-start(bf16[2,2,1024,1024]{3,2,1,0:T(8,128)(2,1)} %refs_4_.3) | copy-start | bytes 25165828
  8.7 5.1 %collective-permute-start.2 = (bf16[2,16,1024]{2,1,0:T(8,128)(2,1)S(1)}, bf16[2,16,1024]{2,1,0:T(8,128)(2,1)S(1)}, u32[]{:S(2)}, u32[]{:S(2)}) collective-permute-start(bf16[2,16,1024]{2,1,0:T(8,128)(2,1)S(1)} %collective-permute-done.refs_0_), channel_id=1, source_target_pairs={{0,8},{8,0},{16,24},{24,16},{1,9},{9,1},{17,25},{25,17},{2,10},{10... | collective-permute-start | bytes 196616 | tf_op jit(solution)/shard_map/ppermute | solution.py:138
  11.0 4.3 %collective-permute-start.5 = (bf16[2,16,1024]{2,1,0:T(8,128)(2,1)S(1)}, bf16[2,16,1024]{2,1,0:T(8,128)(2,1)S(1)}, u32[]{:S(2)}, u32[]{:S(2)}) collective-permute-start(bf16[2,16,1024]{2,1,0:T(8,128)(2,1)S(1)} %collective-permute-done.4.refs_0_), channel_id=1, source_target_pairs={{0,8},{8,0},{16,24},{24,16},{1,9},{9,1},{17,25},{25,17},{2,10},{10... | collective-permute-start | bytes 196616 | tf_op jit(solution)/shard_map/ppermute | solution.py:138
  14.6 1.6 %collective-permute-start.3 = (f32[4,2,8,1024]{3,2,1,0:T(8,128)S(1)}, f32[4,2,8,1024]{3,2,1,0:T(8,128)S(1)}, u32[]{:S(2)}, u32[]{:S(2)}) collective-permute-start(f32[4,2,8,1024]{3,2,1,0:T(8,128)S(1)} %get-tuple-element.16), channel_id=1, source_target_pairs={{0,1},{1,0},{2,3},{3,2},{4,5},{5,4},{6,7},{7,6},{8,9},{9,8},{10,11... | collective-permute-start | bytes 786440 | tf_op jit(solution)/shard_map/ppermute | solution.py:138
  16.0 1.6 %collective-permute-start.6 = (f32[4,2,8,1024]{3,2,1,0:T(8,128)S(1)}, f32[4,2,8,1024]{3,2,1,0:T(8,128)S(1)}, u32[]{:S(2)}, u32[]{:S(2)}) collective-permute-start(f32[4,2,8,1024]{3,2,1,0:T(8,128)S(1)} %get-tuple-element.18), channel_id=1, source_target_pairs={{0,1},{1,0},{2,3},{3,2},{4,5},{5,4},{6,7},{7,6},{8,9},{9,8},{10,11... | collective-permute-start | bytes 786440 | tf_op jit(solution)/shard_map/ppermute | solution.py:138
  17.7 6.8 %collective-permute-start.7 = (f32[4,8,1024]{2,1,0:T(8,128)S(1)}, f32[4,8,1024]{2,1,0:T(8,128)S(1)}, u32[]{:S(2)}, u32[]{:S(2)}) collective-permute-start(f32[4,8,1024]{2,1,0:T(8,128)S(1)} %get-tuple-element.20), channel_id=1, source_target_pairs={{0,6},{1,7},{2,4},{3,5},{4,2},{5,3},{6,0},{7,1},{8,14},{9,15},{10,... | collective-permute-start | bytes 393224 | tf_op jit(solution)/shard_map/ppermute | solution.py:138
  20.6 6.6 %collective-permute-start.8 = (f32[4,8,1024]{2,1,0:T(8,128)S(1)}, f32[4,8,1024]{2,1,0:T(8,128)S(1)}, u32[]{:S(2)}, u32[]{:S(2)}) collective-permute-start(f32[4,8,1024]{2,1,0:T(8,128)S(1)} %get-tuple-element.21), channel_id=1, source_target_pairs={{0,4},{1,5},{2,6},{3,7},{4,0},{5,1},{6,2},{7,3},{8,12},{9,13},{10,... | collective-permute-start | bytes 393224 | tf_op jit(solution)/shard_map/ppermute | solution.py:138
  21.1 6.4 %collective-permute-start.9 = (f32[4,8,1024]{2,1,0:T(8,128)S(1)}, f32[4,8,1024]{2,1,0:T(8,128)S(1)}, u32[]{:S(2)}, u32[]{:S(2)}) collective-permute-start(f32[4,8,1024]{2,1,0:T(8,128)S(1)} %get-tuple-element.22), channel_id=1, source_target_pairs={{0,2},{1,3},{2,0},{3,1},{4,6},{5,7},{6,4},{7,5},{8,10},{9,11},{10,... | collective-permute-start | bytes 393224 | tf_op jit(solution)/shard_map/ppermute | solution.py:138

commit v4 on v3

--- a/solution.py
+++ b/solution.py
@@ -72,13 +72,17 @@
 def gate_kernel(parts, weight_ref, *refs):
     pieces, out_ref = refs[:parts], refs[parts]
     held_ref, sems = refs[parts + 1 :]
-    terms, rows, width = pieces[0].shape
-    gates = out_ref.shape[0]
+    gates, terms, _ = weight_ref.shape
+    _, rows, width = out_ref.shape
     blocks = [slice(at, at + LANES) for at in range(0, width, LANES)]
+    whole = [piece for piece in pieces if piece.shape[0] == terms]
+    split = [piece for piece in pieces if piece.shape[0] != terms]
     total = []
     for t in range(terms):
-        whole = sum(piece[t] for piece in pieces[1:]) + pieces[0][t]
-        total.append([whole[:, block] for block in blocks])
+        value = sum(piece[t] for piece in whole)
+        if split:
+            value += split[t // 2][t % 2]
+        total.append([value[:, block] for block in blocks])
     copies = []
     for at in range(0, gates, GATES_AT_ONCE):
         for g in range(at, at + GATES_AT_ONCE):
@@ -142,15 +146,22 @@
     far = [swap(own[f], "tx", txs // 2) for f in range(freqs)]
     near = swap(lax.optimization_barrier((green, own[-1]))[0], "tx", 1)
     far[0], weights = lax.optimization_barrier((far[0], weights))
-    keeps, gots = [], []
+    beyond = [swap(far[f], "tx", 1) for f in range(freqs)]
+    sums, early = [], []
+    last = chips - 1
     for f in range(freqs):
-        slots = {0: own[f], 1: near, txs // 2: far[f], txs // 2 + 1: swap(far[f], "tx", 1)}
+        slots = {0: own[f], 1: near, txs // 2: far[f], txs // 2 + 1: beyond[f]}
         offsets = [txs // 2, 1, txs // 2 + 1, 0]
         keep, send = responses(f, offsets, [slots[s] for s in offsets], currents, chips)
-        keeps.append(keep)
-        gots.append(swap(send, "cell", 1))
-    sums = jnp.concatenate([keep + got for keep, got in zip(keeps, gots)], 1)
-    pieces = [swap(sums[k], "cell", 2 * k) for k in range(chips - 1, 0, -1)] + [sums[0]]
+        if f:
+            send, sums[-1] = lax.optimization_barrier((send, sums[-1]))
+        size = chips if f == freqs - 1 else max(chips // 4, 1)
+        got = [swap(send[at : at + size], "cell", 1) for at in range(0, chips, size)]
+        sums.append(keep + jnp.concatenate(got))
+    early = [swap(by_freq[last], "cell", 2 * last) for by_freq in sums]
+    sums = jnp.concatenate([by_freq[:last] for by_freq in sums], 1)
+    rest = [swap(sums[k], "cell", 2 * k) for k in range(1, last)] + [sums[0]]
+    pieces = early[:1] + rest + early[1:]
     return gates_of(weights, pieces)
 
 

time: 29.1 us -> 28.4 us (0.976)
  waiting for transfers between devices: 10.9 us -> 6.25 us
  starting transfers between devices: 13.1 us -> 16.9 us
    ppermute x10 -> x14, waiting for transfers between devices: 10.9 us -> 6.25 us  [swap(): lax.ppermute(a, axis, [(i, i ^ bit) for i in range({'tx': txs, 'cell': ce...]
    ppermute x10 -> x14, starting transfers between devices: 13.1 us -> 16.9 us  [swap(): lax.ppermute(a, axis, [(i, i ^ bit) for i in range({'tx': txs, 'cell': ce...]
  transfers between devices with their start and end apart: 10 -> 14, of which waited for: 9 -> 6; matrix products, arithmetic and copies ran while one was open for 3% -> 4% of each run, Pallas kernels for 5% -> 6%
where the time goes in v4:
time: 28.4 us; the launch traced here: 28.2 us
  starting transfers between devices  16.9 us (60%)
  waiting for transfers between devices  6.25 us (22%)
  Pallas kernels  3.02 us (11%)
  local copies, waits for them, and re-layouts  1.04 us (4%)
  other arithmetic  0.89 us (3%)
    ppermute x14, starting transfers between devices, swap(): lax.ppermute(a, axis, [(i, i ^ bit) for i in range({'tx': txs, 'cell': ce...  16.9 us
    ppermute x14, waiting for transfers between devices, swap(): lax.ppermute(a, axis, [(i, i ^ bit) for i in range({'tx': txs, 'cell': ce...  6.25 us
    pallas_call x1, Pallas kernels, gates_of(): pl.pallas_call(functools.partial(gate_kernel, len(pieces)), out_shape=jax...  1.45 us
    pallas_call x2, Pallas kernels, responses(): pl.pallas_call(functools.partial(response_kernel, freq, offsets, chips),...  1.45 us
    squeeze x1, local copies, waits for them, and re-layouts, per_device(): own = [green[:, f] for f in range(freqs)]  0.88 us
    cos x1, other arithmetic, per_device(): jnp.cos(gate_phase)  0.78 us
  transfers between devices with their start and end apart: 14, of which 6 were waited for; matrix products, arithmetic and copies ran while one was open for 4% of the time, Pallas kernels for 6%

profile of v4, /device:TPU:0, one launch (start us, length us, event | category | flops | bytes accessed | tf_op | source)
XLA Modules:
  0.0 28.2 jit_solution(2093049776709401024)
XLA Ops:
  0.0 0.9 %slice_bitcast_fusion.2 = (bf16[2,16,1024]{2,1,0:T(8,128)(2,1)S(1)}, bf16[2,16,1024]{2,1,0:T(8,128)(2,1)S(1)}) fusion(bf16[2,2,16,1024]{3,2,1,0:T(8,128)(2,1)} %param.5), kind=kLoop, calls=%fused_computation.13 | loop fusion | bytes 262144 | tf_op jit(solution)/shard_map/squeeze | solution.py:145
  0.9 4.1 %collective-permute-start = (bf16[2,16,1024]{2,1,0:T(8,128)(2,1)S(1)}, bf16[2,16,1024]{2,1,0:T(8,128)(2,1)S(1)}, u32[]{:S(2)}, u32[]{:S(2)}) collective-permute-start(bf16[2,16,1024]{2,1,0:T(8,128)(2,1)S(1)} %get-tuple-element.31.refs_3_), channel_id=1, source_target_pairs={{0,16},{8,24},{16,0},{24,8},{1,17},{9,25},{17,1},{25,9},{2,18},{10... | collective-permute-start | bytes 196616 | tf_op jit(solution)/shard_map/ppermute | solution.py:142
  5.0 0.1 collective-permute-start.1
  5.1 1.8 %collective-permute-start.2 = (bf16[2,2,16,1024]{3,2,1,0:T(8,128)(2,1)}, bf16[2,2,16,1024]{3,2,1,0:T(8,128)(2,1)S(1)}, u32[]{:S(2)}, u32[]{:S(2)}) collective-permute-start(bf16[2,2,16,1024]{3,2,1,0:T(8,128)(2,1)} %param.5), channel_id=1, source_target_pairs={{0,8},{8,0},{16,24},{24,16},{1,9},{9,1},{17,25},{25,17},{2,10},{10... | collective-permute-start | bytes 393224 | tf_op jit(solution)/shard_map/ppermute | solution.py:142
  6.9 0.8 %multiply_cosine_fusion = (f32[64,2,1]{0,1,2:T(2,128)S(1)}, f32[64,2,1]{0,1,2:T(2,128)S(1)}) fusion(f32[64]{0:T(128)} %param.7, f32[2]{0:T(128)} %param.6), kind=kLoop, calls=%fused_computation.17 | loop fusion | flops 256 | bytes 1288 | tf_op jit(solution)/shard_map/cos | solution.py:139
  7.7 0.1 copy.12.weight_ref
  7.8 0.0 copy-start
  7.8 0.1 weights.1.weight_ref
  7.9 0.8 %collective-permute-done.refs_0_ = bf16[2,16,1024]{2,1,0:T(8,128)(2,1)S(1)} collective-permute-done((bf16[2,16,1024]{2,1,0:T(8,128)(2,1)S(1)}, bf16[2,16,1024]{2,1,0:T(8,128)(2,1)S(1)}, u32[]{:S(2)}, u32[]{:S(2)}) %collective-permute-start) | collective-permute-done | bytes 65568 | tf_op jit(solution)/shard_map/ppermute | solution.py:142
  8.7 1.9 %collective-permute-start.4 = (bf16[2,16,1024]{2,1,0:T(8,128)(2,1)S(1)}, bf16[2,16,1024]{2,1,0:T(8,128)(2,1)S(1)}, u32[]{:S(2)}, u32[]{:S(2)}) collective-permute-start(bf16[2,16,1024]{2,1,0:T(8,128)(2,1)S(1)} %collective-permute-done.refs_0_), channel_id=1, source_target_pairs={{0,8},{8,0},{16,24},{24,16},{1,9},{9,1},{17,25},{25,17},{2,10},{10... | collective-permute-start | bytes 196616 | tf_op jit(solution)/shard_map/ppermute | solution.py:142
  10.6 0.3 %collective-permute-done.1.refs_0_ = bf16[2,16,1024]{2,1,0:T(8,128)(2,1)S(1)} collective-permute-done((bf16[2,16,1024]{2,1,0:T(8,128)(2,1)S(1)}, bf16[2,16,1024]{2,1,0:T(8,128)(2,1)S(1)}, u32[]{:S(2)}, u32[]{:S(2)}) %collective-permute-start.1) | collective-permute-done | bytes 65568 | tf_op jit(solution)/shard_map/ppermute | solution.py:142
  11.0 1.5 %collective-permute-start.3 = (bf16[2,16,1024]{2,1,0:T(8,128)(2,1)S(1)}, bf16[2,16,1024]{2,1,0:T(8,128)(2,1)S(1)}, u32[]{:S(2)}, u32[]{:S(2)}) collective-permute-start(bf16[2,16,1024]{2,1,0:T(8,128)(2,1)S(1)} %collective-permute-done.1.refs_0_), channel_id=1, source_target_pairs={{0,8},{8,0},{16,24},{24,16},{1,9},{9,1},{17,25},{25,17},{2,10},{10... | collective-permute-start | bytes 196616 | tf_op jit(solution)/shard_map/ppermute | solution.py:142
  12.4 1.5 %collective-permute-done.4.refs_2_ = bf16[2,16,1024]{2,1,0:T(8,128)(2,1)S(1)} collective-permute-done((bf16[2,16,1024]{2,1,0:T(8,128)(2,1)S(1)}, bf16[2,16,1024]{2,1,0:T(8,128)(2,1)S(1)}, u32[]{:S(2)}, u32[]{:S(2)}) %collective-permute-start.4) | collective-permute-done | bytes 65568 | tf_op jit(solution)/shard_map/ppermute | solution.py:142
  13.9 0.0 collective-permute-done.2.refs_1_
  13.9 0.0 copy-done
  13.9 0.7 %responses.3 = (f32[4,2,8,1024]{3,2,1,0:T(8,128)S(1)}, f32[4,2,8,1024]{3,2,1,0:T(8,128)S(1)}) custom-call(bf16[2,16,1024]{2,1,0:T(8,128)(2,1)S(1)} %collective-permute-done.refs_0_, bf16[2,2,16,1024]{3,2,1,0:T(8,128)(2,1)S(1)} %collective-permute-done.2.refs_1_, bf16[2,16,1024]{2,1,0:T(8,128)(2,1)S(1)} %collective-permute-done.4.refs_2_, ...), custom_call_target="tpu_custom_call" | custom-call | flops 536870912 | bytes 4194304 | tf_op jit(solution)/shard_map/responses/pallas_call | solution.py:60
  14.6 0.1 collective-permute-start.5
  14.7 0.5 %collective-permute-start.8 = (f32[1,2,8,1024]{3,2,1,0:T(8,128)S(1)}, f32[1,2,8,1024]{3,2,1,0:T(8,128)S(1)}, u32[]{:S(2)}, u32[]{:S(2)}) collective-permute-start(f32[1,2,8,1024]{3,2,1,0:T(8,128)S(1)} %get-tuple-element.27), channel_id=1, source_target_pairs={{0,1},{1,0},{2,3},{3,2},{4,5},{5,4},{6,7},{7,6},{8,9},{9,8},{10,11... | collective-permute-start | bytes 196616 | tf_op jit(solution)/shard_map/ppermute | solution.py:142
  15.2 0.1 collective-permute-start.7
  15.3 0.4 %collective-permute-start.6 = (f32[1,2,8,1024]{3,2,1,0:T(8,128)S(1)}, f32[1,2,8,1024]{3,2,1,0:T(8,128)S(1)}, u32[]{:S(2)}, u32[]{:S(2)}) collective-permute-start(f32[1,2,8,1024]{3,2,1,0:T(8,128)S(1)} %get-tuple-element.29), channel_id=1, source_target_pairs={{0,1},{1,0},{2,3},{3,2},{4,5},{5,4},{6,7},{7,6},{8,9},{9,8},{10,11... | collective-permute-start | bytes 196616 | tf_op jit(solution)/shard_map/ppermute | solution.py:142
  15.7 0.0 collective-permute-done.3.refs_2_
  15.7 0.7 %responses.2 = (f32[4,2,8,1024]{3,2,1,0:T(8,128)S(1)}, f32[4,2,8,1024]{3,2,1,0:T(8,128)S(1)}) custom-call(bf16[2,16,1024]{2,1,0:T(8,128)(2,1)S(1)} %collective-permute-done.1.refs_0_, bf16[2,2,16,1024]{3,2,1,0:T(8,128)(2,1)S(1)} %collective-permute-done.2.refs_1_, bf16[2,16,1024]{2,1,0:T(8,128)(2,1)S(1)} %collective-permute-done.3.refs_2_, ...), custom_call_target="tpu_custom_call" | custom-call | flops 536870912 | bytes 4194304 | tf_op jit(solution)/shard_map/responses/pallas_call | solution.py:60
  16.5 0.0 collective-permute-done.5
  16.5 0.0 collective-permute-done.8
  16.5 0.0 collective-permute-done.7
  16.5 0.1 collective-permute-done.6
  16.7 0.4 %collective-permute-start.10 = (f32[4,2,8,1024]{3,2,1,0:T(8,128)S(1)}, f32[4,2,8,1024]{3,2,1,0:T(8,128)S(1)}, u32[]{:S(2)}, u32[]{:S(2)}) collective-permute-start(f32[4,2,8,1024]{3,2,1,0:T(8,128)S(1)} %get-tuple-element.22), channel_id=1, source_target_pairs={{0,1},{1,0},{2,3},{3,2},{4,5},{5,4},{6,7},{7,6},{8,9},{9,8},{10,11... | collective-permute-start | bytes 786440 | tf_op jit(solution)/shard_map/ppermute | solution.py:142
  17.1 2.5 %collective-permute-start.9 = (f32[2,8,1024]{2,1,0:T(8,128)S(1)}, f32[2,8,1024]{2,1,0:T(8,128)S(1)}, u32[]{:S(2)}, u32[]{:S(2)}) collective-permute-start(f32[2,8,1024]{2,1,0:T(8,128)S(1)} %slice_bitcast_fusion.1), channel_id=1, source_target_pairs={{0,6},{1,7},{2,4},{3,5},{4,2},{5,3},{6,0},{7,1},{8,14},{9,15},{10,... | collective-permute-start | bytes 196616 | tf_op jit(solution)/shard_map/ppermute | solution.py:142
  19.6 0.0 collective-permute-done.10
  19.7 0.6 %collective-permute-start.11 = (f32[4,8,1024]{2,1,0:T(8,128)S(1)}, f32[4,8,1024]{2,1,0:T(8,128)S(1)}, u32[]{:S(2)}, u32[]{:S(2)}) collective-permute-start(f32[4,8,1024]{2,1,0:T(8,128)S(1)} %get-tuple-element.24), channel_id=1, source_target_pairs={{0,2},{1,3},{2,0},{3,1},{4,6},{5,7},{6,4},{7,5},{8,10},{9,11},{10,... | collective-permute-start | bytes 393224 | tf_op jit(solution)/shard_map/ppermute | solution.py:142
  20.3 1.1 %collective-permute-start.12 = (f32[4,8,1024]{2,1,0:T(8,128)S(1)}, f32[4,8,1024]{2,1,0:T(8,128)S(1)}, u32[]{:S(2)}, u32[]{:S(2)}) collective-permute-start(f32[4,8,1024]{2,1,0:T(8,128)S(1)} %get-tuple-element.25), channel_id=1, source_target_pairs={{0,4},{1,5},{2,6},{3,7},{4,0},{5,1},{6,2},{7,3},{8,12},{9,13},{10,... | collective-permute-start | bytes 393224 | tf_op jit(solution)/shard_map/ppermute | solution.py:142
  21.4 1.8 %collective-permute-start.13 = (f32[2,8,1024]{2,1,0:T(8,128)S(1)}, f32[2,8,1024]{2,1,0:T(8,128)S(1)}, u32[]{:S(2)}, u32[]{:S(2)}) collective-permute-start(f32[2,8,1024]{2,1,0:T(8,128)S(1)} %slice_bitcast_fusion), channel_id=1, source_target_pairs={{0,6},{1,7},{2,4},{3,5},{4,2},{5,3},{6,0},{7,1},{8,14},{9,15},{10,... | collective-permute-start | bytes 196616 | tf_op jit(solution)/shard_map/ppermute | solution.py:142
  23.2 0.0 collective-permute-done.9.refs_0_
  23.2 3.4 %collective-permute-done.13.refs_4_ = f32[2,8,1024]{2,1,0:T(8,128)S(1)} collective-permute-done((f32[2,8,1024]{2,1,0:T(8,128)S(1)}, f32[2,8,1024]{2,1,0:T(8,128)S(1)}, u32[]{:S(2)}, u32[]{:S(2)}) %collective-permute-start.13) | collective-permute-done | bytes 65568 | tf_op jit(solution)/shard_map/ppermute | solution.py:142
  26.7 0.0 collective-permute-done.11.refs_1_
  26.7 0.1 collective-permute-done.12.refs_2_
  26.7 1.5 %gates.1 = f32[64,8,1024]{2,1,0:T(8,128)} custom-call(f32[64,4,128]{2,1,0:T(4,128)S(1)} %weights.1.weight_ref, f32[2,8,1024]{2,1,0:T(8,128)S(1)} %collective-permute-done.9.refs_0_, f32[4,8,1024]{2,1,0:T(8,128)S(1)} %collective-permute-done.11.refs_1_, f32[4,8,1024]{2,1,0:T(8,128)S(1)} %collective-permute-done.12.refs_2_, ...), custom_call_target="tpu_custom_call" | custom-call | tf_op jit(solution)/shard_map/gates/pallas_call | solution.py:106
  (10 shorter events, 0.2 us)
Async XLA Ops:
  0.9 7.9 %collective-permute-start = (bf16[2,16,1024]{2,1,0:T(8,128)(2,1)S(1)}, bf16[2,16,1024]{2,1,0:T(8,128)(2,1)S(1)}, u32[]{:S(2)}, u32[]{:S(2)}) collective-permute-start(bf16[2,16,1024]{2,1,0:T(8,128)(2,1)S(1)} %get-tuple-element.31.refs_3_), channel_id=1, source_target_pairs={{0,16},{8,24},{16,0},{24,8},{1,17},{9,25},{17,1},{25,9},{2,18},{10... | collective-permute-start | bytes 196616 | tf_op jit(solution)/shard_map/ppermute | solution.py:142
  5.0 6.0 %collective-permute-start.1 = (bf16[2,16,1024]{2,1,0:T(8,128)(2,1)S(1)}, bf16[2,16,1024]{2,1,0:T(8,128)(2,1)S(1)}, u32[]{:S(2)}, u32[]{:S(2)}) collective-permute-start(bf16[2,16,1024]{2,1,0:T(8,128)(2,1)S(1)} %get-tuple-element.30.refs_3_), channel_id=1, source_target_pairs={{0,16},{8,24},{16,0},{24,8},{1,17},{9,25},{17,1},{25,9},{2,18},{10... | collective-permute-start | bytes 196616 | tf_op jit(solution)/shard_map/ppermute | solution.py:142
  5.1 8.8 %collective-permute-start.2 = (bf16[2,2,16,1024]{3,2,1,0:T(8,128)(2,1)}, bf16[2,2,16,1024]{3,2,1,0:T(8,128)(2,1)S(1)}, u32[]{:S(2)}, u32[]{:S(2)}) collective-permute-start(bf16[2,2,16,1024]{3,2,1,0:T(8,128)(2,1)} %param.5), channel_id=1, source_target_pairs={{0,8},{8,0},{16,24},{24,16},{1,9},{9,1},{17,25},{25,17},{2,10},{10... | collective-permute-start | bytes 393224 | tf_op jit(solution)/shard_map/ppermute | solution.py:142
  7.8 6.1 %copy-start = (bf16[2,2,1024,1024]{3,2,1,0:T(8,128)(2,1)S(1)}, bf16[2,2,1024,1024]{3,2,1,0:T(8,128)(2,1)}, u32[]{:S(2)}) copy-start(bf16[2,2,1024,1024]{3,2,1,0:T(8,128)(2,1)} %refs_4_.3) | copy-start | bytes 25165828
  8.7 5.1 %collective-permute-start.4 = (bf16[2,16,1024]{2,1,0:T(8,128)(2,1)S(1)}, bf16[2,16,1024]{2,1,0:T(8,128)(2,1)S(1)}, u32[]{:S(2)}, u32[]{:S(2)}) collective-permute-start(bf16[2,16,1024]{2,1,0:T(8,128)(2,1)S(1)} %collective-permute-done.refs_0_), channel_id=1, source_target_pairs={{0,8},{8,0},{16,24},{24,16},{1,9},{9,1},{17,25},{25,17},{2,10},{10... | collective-permute-start | bytes 196616 | tf_op jit(solution)/shard_map/ppermute | solution.py:142
  11.0 4.8 %collective-permute-start.3 = (bf16[2,16,1024]{2,1,0:T(8,128)(2,1)S(1)}, bf16[2,16,1024]{2,1,0:T(8,128)(2,1)S(1)}, u32[]{:S(2)}, u32[]{:S(2)}) collective-permute-start(bf16[2,16,1024]{2,1,0:T(8,128)(2,1)S(1)} %collective-permute-done.1.refs_0_), channel_id=1, source_target_pairs={{0,8},{8,0},{16,24},{24,16},{1,9},{9,1},{17,25},{25,17},{2,10},{10... | collective-permute-start | bytes 196616 | tf_op jit(solution)/shard_map/ppermute | solution.py:142
  14.6 1.8 %collective-permute-start.5 = (f32[1,2,8,1024]{3,2,1,0:T(8,128)S(1)}, f32[1,2,8,1024]{3,2,1,0:T(8,128)S(1)}, u32[]{:S(2)}, u32[]{:S(2)}) collective-permute-start(f32[1,2,8,1024]{3,2,1,0:T(8,128)S(1)} %get-tuple-element.26), channel_id=1, source_target_pairs={{0,1},{1,0},{2,3},{3,2},{4,5},{5,4},{6,7},{7,6},{8,9},{9,8},{10,11... | collective-permute-start | bytes 196616 | tf_op jit(solution)/shard_map/ppermute | solution.py:142
  14.7 1.8 %collective-permute-start.8 = (f32[1,2,8,1024]{3,2,1,0:T(8,128)S(1)}, f32[1,2,8,1024]{3,2,1,0:T(8,128)S(1)}, u32[]{:S(2)}, u32[]{:S(2)}) collective-permute-start(f32[1,2,8,1024]{3,2,1,0:T(8,128)S(1)} %get-tuple-element.27), channel_id=1, source_target_pairs={{0,1},{1,0},{2,3},{3,2},{4,5},{5,4},{6,7},{7,6},{8,9},{9,8},{10,11... | collective-permute-start | bytes 196616 | tf_op jit(solution)/shard_map/ppermute | solution.py:142
  15.2 1.3 %collective-permute-start.7 = (f32[1,2,8,1024]{3,2,1,0:T(8,128)S(1)}, f32[1,2,8,1024]{3,2,1,0:T(8,128)S(1)}, u32[]{:S(2)}, u32[]{:S(2)}) collective-permute-start(f32[1,2,8,1024]{3,2,1,0:T(8,128)S(1)} %get-tuple-element.28), channel_id=1, source_target_pairs={{0,1},{1,0},{2,3},{3,2},{4,5},{5,4},{6,7},{7,6},{8,9},{9,8},{10,11... | collective-permute-start | bytes 196616 | tf_op jit(solution)/shard_map/ppermute | solution.py:142
  15.3 1.3 %collective-permute-start.6 = (f32[1,2,8,1024]{3,2,1,0:T(8,128)S(1)}, f32[1,2,8,1024]{3,2,1,0:T(8,128)S(1)}, u32[]{:S(2)}, u32[]{:S(2)}) collective-permute-start(f32[1,2,8,1024]{3,2,1,0:T(8,128)S(1)} %get-tuple-element.29), channel_id=1, source_target_pairs={{0,1},{1,0},{2,3},{3,2},{4,5},{5,4},{6,7},{7,6},{8,9},{9,8},{10,11... | collective-permute-start | bytes 196616 | tf_op jit(solution)/shard_map/ppermute | solution.py:142
  16.7 2.9 %collective-permute-start.10 = (f32[4,2,8,1024]{3,2,1,0:T(8,128)S(1)}, f32[4,2,8,1024]{3,2,1,0:T(8,128)S(1)}, u32[]{:S(2)}, u32[]{:S(2)}) collective-permute-start(f32[4,2,8,1024]{3,2,1,0:T(8,128)S(1)} %get-tuple-element.22), channel_id=1, source_target_pairs={{0,1},{1,0},{2,3},{3,2},{4,5},{5,4},{6,7},{7,6},{8,9},{9,8},{10,11... | collective-permute-start | bytes 786440 | tf_op jit(solution)/shard_map/ppermute | solution.py:142
  17.1 6.1 %collective-permute-start.9 = (f32[2,8,1024]{2,1,0:T(8,128)S(1)}, f32[2,8,1024]{2,1,0:T(8,128)S(1)}, u32[]{:S(2)}, u32[]{:S(2)}) collective-permute-start(f32[2,8,1024]{2,1,0:T(8,128)S(1)} %slice_bitcast_fusion.1), channel_id=1, source_target_pairs={{0,6},{1,7},{2,4},{3,5},{4,2},{5,3},{6,0},{7,1},{8,14},{9,15},{10,... | collective-permute-start | bytes 196616 | tf_op jit(solution)/shard_map/ppermute | solution.py:142
  19.7 7.0 %collective-permute-start.11 = (f32[4,8,1024]{2,1,0:T(8,128)S(1)}, f32[4,8,1024]{2,1,0:T(8,128)S(1)}, u32[]{:S(2)}, u32[]{:S(2)}) collective-permute-start(f32[4,8,1024]{2,1,0:T(8,128)S(1)} %get-tuple-element.24), channel_id=1, source_target_pairs={{0,2},{1,3},{2,0},{3,1},{4,6},{5,7},{6,4},{7,5},{8,10},{9,11},{10,... | collective-permute-start | bytes 393224 | tf_op jit(solution)/shard_map/ppermute | solution.py:142
  20.3 6.5 %collective-permute-start.12 = (f32[4,8,1024]{2,1,0:T(8,128)S(1)}, f32[4,8,1024]{2,1,0:T(8,128)S(1)}, u32[]{:S(2)}, u32[]{:S(2)}) collective-permute-start(f32[4,8,1024]{2,1,0:T(8,128)S(1)} %get-tuple-element.25), channel_id=1, source_target_pairs={{0,4},{1,5},{2,6},{3,7},{4,0},{5,1},{6,2},{7,3},{8,12},{9,13},{10,... | collective-permute-start | bytes 393224 | tf_op jit(solution)/shard_map/ppermute | solution.py:142
  21.4 5.3 %collective-permute-start.13 = (f32[2,8,1024]{2,1,0:T(8,128)S(1)}, f32[2,8,1024]{2,1,0:T(8,128)S(1)}, u32[]{:S(2)}, u32[]{:S(2)}) collective-permute-start(f32[2,8,1024]{2,1,0:T(8,128)S(1)} %slice_bitcast_fusion), channel_id=1, source_target_pairs={{0,6},{1,7},{2,4},{3,5},{4,2},{5,3},{6,0},{7,1},{8,14},{9,15},{10,... | collective-permute-start | bytes 196616 | tf_op jit(solution)/shard_map/ppermute | solution.py:142

commit v5 on v4

--- a/solution.py
+++ b/solution.py
@@ -149,17 +149,21 @@
     beyond = [swap(far[f], "tx", 1) for f in range(freqs)]
     sums, early = [], []
     last = chips - 1
+    offsets = [txs // 2, 1, txs // 2 + 1, 0]
     for f in range(freqs):
         slots = {0: own[f], 1: near, txs // 2: far[f], txs // 2 + 1: beyond[f]}
-        offsets = [txs // 2, 1, txs // 2 + 1, 0]
         keep, send = responses(f, offsets, [slots[s] for s in offsets], currents, chips)
-        if f:
-            send, sums[-1] = lax.optimization_barrier((send, sums[-1]))
-        size = chips if f == freqs - 1 else max(chips // 4, 1)
-        got = [swap(send[at : at + size], "cell", 1) for at in range(0, chips, size)]
-        sums.append(keep + jnp.concatenate(got))
-    early = [swap(by_freq[last], "cell", 2 * last) for by_freq in sums]
-    sums = jnp.concatenate([by_freq[:last] for by_freq in sums], 1)
+        if f < freqs - 1:
+            size = max(chips // 4, 1)
+            got = [swap(send[at : min(at + size, last)], "cell", 1) for at in range(0, last, size)]
+            early.append(keep[last] + swap(send[last], "cell", 1))
+            sums.append(keep[:last] + jnp.concatenate(got))
+        else:
+            whole = keep + swap(send, "cell", 1)
+            early.append(whole[last])
+            sums.append(whole[:last])
+    early = [swap(farthest, "cell", 2 * last) for farthest in early]
+    sums = jnp.concatenate(sums, 1)
     rest = [swap(sums[k], "cell", 2 * k) for k in range(1, last)] + [sums[0]]
     pieces = early[:1] + rest + early[1:]
     return gates_of(weights, pieces)

time: 28.4 us -> 28.2 us (level)
  starting transfers between devices: 16.9 us -> 16.6 us
  transfers between devices with their start and end apart: 14 -> 14, of which waited for: 6 -> 5; matrix products, arithmetic and copies ran while one was open for 4% -> 4% of each run, Pallas kernels for 6% -> 6%
where the time goes in v5:
time: 28.2 us; the launch traced here: 28 us
  starting transfers between devices  16.6 us (59%)
  waiting for transfers between devices  6.34 us (22%)
  Pallas kernels  3.02 us (11%)
  local copies, waits for them, and re-layouts  1.02 us (4%)
  other arithmetic  0.88 us (3%)
    ppermute x14, starting transfers between devices, swap(): lax.ppermute(a, axis, [(i, i ^ bit) for i in range({'tx': txs, 'cell': ce...  16.6 us
    ppermute x14, waiting for transfers between devices, swap(): lax.ppermute(a, axis, [(i, i ^ bit) for i in range({'tx': txs, 'cell': ce...  6.34 us
    pallas_call x1, Pallas kernels, gates_of(): pl.pallas_call(functools.partial(gate_kernel, len(pieces)), out_shape=jax...  1.45 us
    pallas_call x2, Pallas kernels, responses(): pl.pallas_call(functools.partial(response_kernel, freq, offsets, chips),...  1.45 us
    squeeze x1, local copies, waits for them, and re-layouts, per_device(): own = [green[:, f] for f in range(freqs)]  0.88 us
    cos x1, other arithmetic, per_device(): jnp.cos(gate_phase)  0.78 us
  transfers between devices with their start and end apart: 14, of which 5 were waited for; matrix products, arithmetic and copies ran while one was open for 4% of the time, Pallas kernels for 6%

profile of v5, /device:TPU:0, one launch (start us, length us, event | category | flops | bytes accessed | tf_op | source)
XLA Modules:
  0.0 28.0 jit_solution(7795300524167003301)
XLA Ops:
  0.0 0.9 %slice_bitcast_fusion.2 = (bf16[2,16,1024]{2,1,0:T(8,128)(2,1)S(1)}, bf16[2,16,1024]{2,1,0:T(8,128)(2,1)S(1)}) fusion(bf16[2,2,16,1024]{3,2,1,0:T(8,128)(2,1)} %param.5), kind=kLoop, calls=%fused_computation.14 | loop fusion | bytes 262144 | tf_op jit(solution)/shard_map/squeeze | solution.py:145
  0.9 4.1 %collective-permute-start = (bf16[2,16,1024]{2,1,0:T(8,128)(2,1)S(1)}, bf16[2,16,1024]{2,1,0:T(8,128)(2,1)S(1)}, u32[]{:S(2)}, u32[]{:S(2)}) collective-permute-start(bf16[2,16,1024]{2,1,0:T(8,128)(2,1)S(1)} %get-tuple-element.27.refs_3_), channel_id=1, source_target_pairs={{0,16},{8,24},{16,0},{24,8},{1,17},{9,25},{17,1},{25,9},{2,18},{10... | collective-permute-start | bytes 196616 | tf_op jit(solution)/shard_map/ppermute | solution.py:142
  5.0 0.1 collective-permute-start.8
  5.1 1.8 %collective-permute-start.1 = (bf16[2,2,16,1024]{3,2,1,0:T(8,128)(2,1)}, bf16[2,2,16,1024]{3,2,1,0:T(8,128)(2,1)S(1)}, u32[]{:S(2)}, u32[]{:S(2)}) collective-permute-start(bf16[2,2,16,1024]{3,2,1,0:T(8,128)(2,1)} %param.5), channel_id=1, source_target_pairs={{0,8},{8,0},{16,24},{24,16},{1,9},{9,1},{17,25},{25,17},{2,10},{10... | collective-permute-start | bytes 393224 | tf_op jit(solution)/shard_map/ppermute | solution.py:142
  6.9 0.8 %multiply_cosine_fusion = (f32[64,2,1]{0,1,2:T(2,128)S(1)}, f32[64,2,1]{0,1,2:T(2,128)S(1)}) fusion(f32[64]{0:T(128)} %param.7, f32[2]{0:T(128)} %param.6), kind=kLoop, calls=%fused_computation.18 | loop fusion | flops 256 | bytes 1288 | tf_op jit(solution)/shard_map/cos | solution.py:139
  7.7 0.1 copy.12.weight_ref
  7.8 0.0 copy-start
  7.8 0.1 weights.1.weight_ref
  7.9 0.8 %collective-permute-done.refs_0_ = bf16[2,16,1024]{2,1,0:T(8,128)(2,1)S(1)} collective-permute-done((bf16[2,16,1024]{2,1,0:T(8,128)(2,1)S(1)}, bf16[2,16,1024]{2,1,0:T(8,128)(2,1)S(1)}, u32[]{:S(2)}, u32[]{:S(2)}) %collective-permute-start) | collective-permute-done | bytes 65568 | tf_op jit(solution)/shard_map/ppermute | solution.py:142
  8.7 1.9 %collective-permute-start.2 = (bf16[2,16,1024]{2,1,0:T(8,128)(2,1)S(1)}, bf16[2,16,1024]{2,1,0:T(8,128)(2,1)S(1)}, u32[]{:S(2)}, u32[]{:S(2)}) collective-permute-start(bf16[2,16,1024]{2,1,0:T(8,128)(2,1)S(1)} %collective-permute-done.refs_0_), channel_id=1, source_target_pairs={{0,8},{8,0},{16,24},{24,16},{1,9},{9,1},{17,25},{25,17},{2,10},{10... | collective-permute-start | bytes 196616 | tf_op jit(solution)/shard_map/ppermute | solution.py:142
  10.6 0.3 %collective-permute-done.8.refs_0_ = bf16[2,16,1024]{2,1,0:T(8,128)(2,1)S(1)} collective-permute-done((bf16[2,16,1024]{2,1,0:T(8,128)(2,1)S(1)}, bf16[2,16,1024]{2,1,0:T(8,128)(2,1)S(1)}, u32[]{:S(2)}, u32[]{:S(2)}) %collective-permute-start.8) | collective-permute-done | bytes 65568 | tf_op jit(solution)/shard_map/ppermute | solution.py:142
  11.0 1.5 %collective-permute-start.9 = (bf16[2,16,1024]{2,1,0:T(8,128)(2,1)S(1)}, bf16[2,16,1024]{2,1,0:T(8,128)(2,1)S(1)}, u32[]{:S(2)}, u32[]{:S(2)}) collective-permute-start(bf16[2,16,1024]{2,1,0:T(8,128)(2,1)S(1)} %collective-permute-done.8.refs_0_), channel_id=1, source_target_pairs={{0,8},{8,0},{16,24},{24,16},{1,9},{9,1},{17,25},{25,17},{2,10},{10... | collective-permute-start | bytes 196616 | tf_op jit(solution)/shard_map/ppermute | solution.py:142
  12.4 1.5 %collective-permute-done.2.refs_2_ = bf16[2,16,1024]{2,1,0:T(8,128)(2,1)S(1)} collective-permute-done((bf16[2,16,1024]{2,1,0:T(8,128)(2,1)S(1)}, bf16[2,16,1024]{2,1,0:T(8,128)(2,1)S(1)}, u32[]{:S(2)}, u32[]{:S(2)}) %collective-permute-start.2) | collective-permute-done | bytes 65568 | tf_op jit(solution)/shard_map/ppermute | solution.py:142
  13.9 0.0 collective-permute-done.1.refs_1_
  13.9 0.0 copy-done
  13.9 0.7 %responses.2 = (f32[4,2,8,1024]{3,2,1,0:T(8,128)S(1)}, f32[4,2,8,1024]{3,2,1,0:T(8,128)S(1)}) custom-call(bf16[2,16,1024]{2,1,0:T(8,128)(2,1)S(1)} %collective-permute-done.refs_0_, bf16[2,2,16,1024]{3,2,1,0:T(8,128)(2,1)S(1)} %collective-permute-done.1.refs_1_, bf16[2,16,1024]{2,1,0:T(8,128)(2,1)S(1)} %collective-permute-done.2.refs_2_, ...), custom_call_target="tpu_custom_call" | custom-call | flops 536870912 | bytes 4194304 | tf_op jit(solution)/shard_map/responses/pallas_call | solution.py:60
  14.6 0.1 collective-permute-start.3
  14.7 0.5 %collective-permute-start.5 = (f32[1,2,8,1024]{3,2,1,0:T(8,128)S(1)}, f32[1,2,8,1024]{3,2,1,0:T(8,128)S(1)}, u32[]{:S(2)}, u32[]{:S(2)}) collective-permute-start(f32[1,2,8,1024]{3,2,1,0:T(8,128)S(1)} %get-tuple-element.22), channel_id=1, source_target_pairs={{0,1},{1,0},{2,3},{3,2},{4,5},{5,4},{6,7},{7,6},{8,9},{9,8},{10,11... | collective-permute-start | bytes 196616 | tf_op jit(solution)/shard_map/ppermute | solution.py:142
  15.2 0.1 collective-permute-start.7
  15.3 0.4 %collective-permute-start.6 = (f32[1,2,8,1024]{3,2,1,0:T(8,128)S(1)}, f32[1,2,8,1024]{3,2,1,0:T(8,128)S(1)}, u32[]{:S(2)}, u32[]{:S(2)}) collective-permute-start(f32[1,2,8,1024]{3,2,1,0:T(8,128)S(1)} %get-tuple-element.24), channel_id=1, source_target_pairs={{0,1},{1,0},{2,3},{3,2},{4,5},{5,4},{6,7},{7,6},{8,9},{9,8},{10,11... | collective-permute-start | bytes 196616 | tf_op jit(solution)/shard_map/ppermute | solution.py:142
  15.7 0.0 collective-permute-done.9.refs_2_
  15.7 0.7 %responses.3 = (f32[4,2,8,1024]{3,2,1,0:T(8,128)S(1)}, f32[4,2,8,1024]{3,2,1,0:T(8,128)S(1)}) custom-call(bf16[2,16,1024]{2,1,0:T(8,128)(2,1)S(1)} %collective-permute-done.8.refs_0_, bf16[2,2,16,1024]{3,2,1,0:T(8,128)(2,1)S(1)} %collective-permute-done.1.refs_1_, bf16[2,16,1024]{2,1,0:T(8,128)(2,1)S(1)} %collective-permute-done.9.refs_2_, ...), custom_call_target="tpu_custom_call" | custom-call | flops 536870912 | bytes 4194304 | tf_op jit(solution)/shard_map/responses/pallas_call | solution.py:60
  16.5 0.1 collective-permute-start.10
  16.6 0.0 collective-permute-done.3
  16.6 2.5 %collective-permute-start.4 = (f32[2,8,1024]{2,1,0:T(8,128)S(1)}, f32[2,8,1024]{2,1,0:T(8,128)S(1)}, u32[]{:S(2)}, u32[]{:S(2)}) collective-permute-start(f32[2,8,1024]{2,1,0:T(8,128)S(1)} %bitcast_add_fusion), channel_id=1, source_target_pairs={{0,6},{1,7},{2,4},{3,5},{4,2},{5,3},{6,0},{7,1},{8,14},{9,15},{10,... | collective-permute-start | bytes 196616 | tf_op jit(solution)/shard_map/ppermute | solution.py:142
  19.1 0.0 collective-permute-done.5
  19.1 0.0 collective-permute-done.7
  19.1 0.0 collective-permute-done.6
  19.1 0.0 collective-permute-done.10
  19.2 0.6 %collective-permute-start.11 = (f32[4,8,1024]{2,1,0:T(8,128)S(1)}, f32[4,8,1024]{2,1,0:T(8,128)S(1)}, u32[]{:S(2)}, u32[]{:S(2)}) collective-permute-start(f32[4,8,1024]{2,1,0:T(8,128)S(1)} %get-tuple-element.20), channel_id=1, source_target_pairs={{0,2},{1,3},{2,0},{3,1},{4,6},{5,7},{6,4},{7,5},{8,10},{9,11},{10,... | collective-permute-start | bytes 393224 | tf_op jit(solution)/shard_map/ppermute | solution.py:142
  19.8 1.3 %collective-permute-start.12 = (f32[4,8,1024]{2,1,0:T(8,128)S(1)}, f32[4,8,1024]{2,1,0:T(8,128)S(1)}, u32[]{:S(2)}, u32[]{:S(2)}) collective-permute-start(f32[4,8,1024]{2,1,0:T(8,128)S(1)} %get-tuple-element.21), channel_id=1, source_target_pairs={{0,4},{1,5},{2,6},{3,7},{4,0},{5,1},{6,2},{7,3},{8,12},{9,13},{10,... | collective-permute-start | bytes 393224 | tf_op jit(solution)/shard_map/ppermute | solution.py:142
  21.2 1.6 %collective-permute-start.13 = (f32[2,8,1024]{2,1,0:T(8,128)S(1)}, f32[2,8,1024]{2,1,0:T(8,128)S(1)}, u32[]{:S(2)}, u32[]{:S(2)}) collective-permute-start(f32[2,8,1024]{2,1,0:T(8,128)S(1)} %slice_bitcast_fusion), channel_id=1, source_target_pairs={{0,6},{1,7},{2,4},{3,5},{4,2},{5,3},{6,0},{7,1},{8,14},{9,15},{10,... | collective-permute-start | bytes 196616 | tf_op jit(solution)/shard_map/ppermute | solution.py:142
  22.8 0.0 collective-permute-done.4.refs_0_
  22.8 3.6 %collective-permute-done.13.refs_4_ = f32[2,8,1024]{2,1,0:T(8,128)S(1)} collective-permute-done((f32[2,8,1024]{2,1,0:T(8,128)S(1)}, f32[2,8,1024]{2,1,0:T(8,128)S(1)}, u32[]{:S(2)}, u32[]{:S(2)}) %collective-permute-start.13) | collective-permute-done | bytes 65568 | tf_op jit(solution)/shard_map/ppermute | solution.py:142
  26.4 0.0 collective-permute-done.11.refs_1_
  26.4 0.1 collective-permute-done.12.refs_2_
  26.5 1.5 %gates.1 = f32[64,8,1024]{2,1,0:T(8,128)} custom-call(f32[64,4,128]{2,1,0:T(4,128)S(1)} %weights.1.weight_ref, f32[2,8,1024]{2,1,0:T(8,128)S(1)} %collective-permute-done.4.refs_0_, f32[4,8,1024]{2,1,0:T(8,128)S(1)} %collective-permute-done.11.refs_1_, f32[4,8,1024]{2,1,0:T(8,128)S(1)} %collective-permute-done.12.refs_2_, ...), custom_call_target="tpu_custom_call" | custom-call | tf_op jit(solution)/shard_map/gates/pallas_call | solution.py:106
  (9 shorter events, 0.1 us)
Async XLA Ops:
  0.9 7.9 %collective-permute-start = (bf16[2,16,1024]{2,1,0:T(8,128)(2,1)S(1)}, bf16[2,16,1024]{2,1,0:T(8,128)(2,1)S(1)}, u32[]{:S(2)}, u32[]{:S(2)}) collective-permute-start(bf16[2,16,1024]{2,1,0:T(8,128)(2,1)S(1)} %get-tuple-element.27.refs_3_), channel_id=1, source_target_pairs={{0,16},{8,24},{16,0},{24,8},{1,17},{9,25},{17,1},{25,9},{2,18},{10... | collective-permute-start | bytes 196616 | tf_op jit(solution)/shard_map/ppermute | solution.py:142
  5.0 6.0 %collective-permute-start.8 = (bf16[2,16,1024]{2,1,0:T(8,128)(2,1)S(1)}, bf16[2,16,1024]{2,1,0:T(8,128)(2,1)S(1)}, u32[]{:S(2)}, u32[]{:S(2)}) collective-permute-start(bf16[2,16,1024]{2,1,0:T(8,128)(2,1)S(1)} %get-tuple-element.26.refs_3_), channel_id=1, source_target_pairs={{0,16},{8,24},{16,0},{24,8},{1,17},{9,25},{17,1},{25,9},{2,18},{10... | collective-permute-start | bytes 196616 | tf_op jit(solution)/shard_map/ppermute | solution.py:142
  5.1 8.8 %collective-permute-start.1 = (bf16[2,2,16,1024]{3,2,1,0:T(8,128)(2,1)}, bf16[2,2,16,1024]{3,2,1,0:T(8,128)(2,1)S(1)}, u32[]{:S(2)}, u32[]{:S(2)}) collective-permute-start(bf16[2,2,16,1024]{3,2,1,0:T(8,128)(2,1)} %param.5), channel_id=1, source_target_pairs={{0,8},{8,0},{16,24},{24,16},{1,9},{9,1},{17,25},{25,17},{2,10},{10... | collective-permute-start | bytes 393224 | tf_op jit(solution)/shard_map/ppermute | solution.py:142
  7.8 6.1 %copy-start = (bf16[2,2,1024,1024]{3,2,1,0:T(8,128)(2,1)S(1)}, bf16[2,2,1024,1024]{3,2,1,0:T(8,128)(2,1)}, u32[]{:S(2)}) copy-start(bf16[2,2,1024,1024]{3,2,1,0:T(8,128)(2,1)} %refs_4_.3) | copy-start | bytes 25165828
  8.7 5.1 %collective-permute-start.2 = (bf16[2,16,1024]{2,1,0:T(8,128)(2,1)S(1)}, bf16[2,16,1024]{2,1,0:T(8,128)(2,1)S(1)}, u32[]{:S(2)}, u32[]{:S(2)}) collective-permute-start(bf16[2,16,1024]{2,1,0:T(8,128)(2,1)S(1)} %collective-permute-done.refs_0_), channel_id=1, source_target_pairs={{0,8},{8,0},{16,24},{24,16},{1,9},{9,1},{17,25},{25,17},{2,10},{10... | collective-permute-start | bytes 196616 | tf_op jit(solution)/shard_map/ppermute | solution.py:142
  11.0 4.8 %collective-permute-start.9 = (bf16[2,16,1024]{2,1,0:T(8,128)(2,1)S(1)}, bf16[2,16,1024]{2,1,0:T(8,128)(2,1)S(1)}, u32[]{:S(2)}, u32[]{:S(2)}) collective-permute-start(bf16[2,16,1024]{2,1,0:T(8,128)(2,1)S(1)} %collective-permute-done.8.refs_0_), channel_id=1, source_target_pairs={{0,8},{8,0},{16,24},{24,16},{1,9},{9,1},{17,25},{25,17},{2,10},{10... | collective-permute-start | bytes 196616 | tf_op jit(solution)/shard_map/ppermute | solution.py:142
  14.6 2.0 %collective-permute-start.3 = (f32[2,8,1024]{2,1,0:T(8,128)S(1)}, f32[2,8,1024]{2,1,0:T(8,128)S(1)}, u32[]{:S(2)}, u32[]{:S(2)}) collective-permute-start(f32[2,8,1024]{2,1,0:T(8,128)S(1)} %get-tuple-element.25), channel_id=1, source_target_pairs={{0,1},{1,0},{2,3},{3,2},{4,5},{5,4},{6,7},{7,6},{8,9},{9,8},{10,11... | collective-permute-start | bytes 196616 | tf_op jit(solution)/shard_map/ppermute | solution.py:142
  14.7 4.4 %collective-permute-start.5 = (f32[1,2,8,1024]{3,2,1,0:T(8,128)S(1)}, f32[1,2,8,1024]{3,2,1,0:T(8,128)S(1)}, u32[]{:S(2)}, u32[]{:S(2)}) collective-permute-start(f32[1,2,8,1024]{3,2,1,0:T(8,128)S(1)} %get-tuple-element.22), channel_id=1, source_target_pairs={{0,1},{1,0},{2,3},{3,2},{4,5},{5,4},{6,7},{7,6},{8,9},{9,8},{10,11... | collective-permute-start | bytes 196616 | tf_op jit(solution)/shard_map/ppermute | solution.py:142
  15.2 3.9 %collective-permute-start.7 = (f32[1,2,8,1024]{3,2,1,0:T(8,128)S(1)}, f32[1,2,8,1024]{3,2,1,0:T(8,128)S(1)}, u32[]{:S(2)}, u32[]{:S(2)}) collective-permute-start(f32[1,2,8,1024]{3,2,1,0:T(8,128)S(1)} %get-tuple-element.23), channel_id=1, source_target_pairs={{0,1},{1,0},{2,3},{3,2},{4,5},{5,4},{6,7},{7,6},{8,9},{9,8},{10,11... | collective-permute-start | bytes 196616 | tf_op jit(solution)/shard_map/ppermute | solution.py:142
  15.3 3.8 %collective-permute-start.6 = (f32[1,2,8,1024]{3,2,1,0:T(8,128)S(1)}, f32[1,2,8,1024]{3,2,1,0:T(8,128)S(1)}, u32[]{:S(2)}, u32[]{:S(2)}) collective-permute-start(f32[1,2,8,1024]{3,2,1,0:T(8,128)S(1)} %get-tuple-element.24), channel_id=1, source_target_pairs={{0,1},{1,0},{2,3},{3,2},{4,5},{5,4},{6,7},{7,6},{8,9},{9,8},{10,11... | collective-permute-start | bytes 196616 | tf_op jit(solution)/shard_map/ppermute | solution.py:142
  16.5 2.7 %collective-permute-start.10 = (f32[4,2,8,1024]{3,2,1,0:T(8,128)S(1)}, f32[4,2,8,1024]{3,2,1,0:T(8,128)S(1)}, u32[]{:S(2)}, u32[]{:S(2)}) collective-permute-start(f32[4,2,8,1024]{3,2,1,0:T(8,128)S(1)} %get-tuple-element.18), channel_id=1, source_target_pairs={{0,1},{1,0},{2,3},{3,2},{4,5},{5,4},{6,7},{7,6},{8,9},{9,8},{10,11... | collective-permute-start | bytes 786440 | tf_op jit(solution)/shard_map/ppermute | solution.py:142
  16.6 6.2 %collective-permute-start.4 = (f32[2,8,1024]{2,1,0:T(8,128)S(1)}, f32[2,8,1024]{2,1,0:T(8,128)S(1)}, u32[]{:S(2)}, u32[]{:S(2)}) collective-permute-start(f32[2,8,1024]{2,1,0:T(8,128)S(1)} %bitcast_add_fusion), channel_id=1, source_target_pairs={{0,6},{1,7},{2,4},{3,5},{4,2},{5,3},{6,0},{7,1},{8,14},{9,15},{10,... | collective-permute-start | bytes 196616 | tf_op jit(solution)/shard_map/ppermute | solution.py:142
  19.2 7.2 %collective-permute-start.11 = (f32[4,8,1024]{2,1,0:T(8,128)S(1)}, f32[4,8,1024]{2,1,0:T(8,128)S(1)}, u32[]{:S(2)}, u32[]{:S(2)}) collective-permute-start(f32[4,8,1024]{2,1,0:T(8,128)S(1)} %get-tuple-element.20), channel_id=1, source_target_pairs={{0,2},{1,3},{2,0},{3,1},{4,6},{5,7},{6,4},{7,5},{8,10},{9,11},{10,... | collective-permute-start | bytes 393224 | tf_op jit(solution)/shard_map/ppermute | solution.py:142
  19.8 6.7 %collective-permute-start.12 = (f32[4,8,1024]{2,1,0:T(8,128)S(1)}, f32[4,8,1024]{2,1,0:T(8,128)S(1)}, u32[]{:S(2)}, u32[]{:S(2)}) collective-permute-start(f32[4,8,1024]{2,1,0:T(8,128)S(1)} %get-tuple-element.21), channel_id=1, source_target_pairs={{0,4},{1,5},{2,6},{3,7},{4,0},{5,1},{6,2},{7,3},{8,12},{9,13},{10,... | collective-permute-start | bytes 393224 | tf_op jit(solution)/shard_map/ppermute | solution.py:142
  21.2 5.2 %collective-permute-start.13 = (f32[2,8,1024]{2,1,0:T(8,128)S(1)}, f32[2,8,1024]{2,1,0:T(8,128)S(1)}, u32[]{:S(2)}, u32[]{:S(2)}) collective-permute-start(f32[2,8,1024]{2,1,0:T(8,128)S(1)} %slice_bitcast_fusion), channel_id=1, source_target_pairs={{0,6},{1,7},{2,4},{3,5},{4,2},{5,3},{6,0},{7,1},{8,14},{9,15},{10,... | collective-permute-start | bytes 196616 | tf_op jit(solution)/shard_map/ppermute | solution.py:142

commit v6 on v5

--- a/solution.py
+++ b/solution.py
@@ -142,22 +142,20 @@
         return lax.ppermute(a, axis, [(i, i ^ bit) for i in range({"tx": txs, "cell": cells}[axis])])
 
     freqs = currents.shape[1]
+    far, near = swap(green, "tx", txs // 2), swap(green, "tx", 1)
     own = [green[:, f] for f in range(freqs)]
-    far = [swap(own[f], "tx", txs // 2) for f in range(freqs)]
-    near = swap(lax.optimization_barrier((green, own[-1]))[0], "tx", 1)
-    far[0], weights = lax.optimization_barrier((far[0], weights))
-    beyond = [swap(far[f], "tx", 1) for f in range(freqs)]
+    weights, *own = lax.optimization_barrier((weights, *own))
+    beyond = [swap(own[f], "tx", txs // 2 + 1) for f in range(freqs)]
     sums, early = [], []
     last = chips - 1
     offsets = [txs // 2, 1, txs // 2 + 1, 0]
     for f in range(freqs):
-        slots = {0: own[f], 1: near, txs // 2: far[f], txs // 2 + 1: beyond[f]}
+        slots = {0: green, 1: near, txs // 2: far, txs // 2 + 1: beyond[f]}
         keep, send = responses(f, offsets, [slots[s] for s in offsets], currents, chips)
         if f < freqs - 1:
-            size = max(chips // 4, 1)
-            got = [swap(send[at : min(at + size, last)], "cell", 1) for at in range(0, last, size)]
+            others = swap(send[:last], "cell", 1)
             early.append(keep[last] + swap(send[last], "cell", 1))
-            sums.append(keep[:last] + jnp.concatenate(got))
+            sums.append(keep[:last] + others)
         else:
             whole = keep + swap(send, "cell", 1)
             early.append(whole[last])

time: 28.2 us -> 27.7 us (0.982)
  local copies, waits for them, and re-layouts: 1.02 us -> 0.16 us
  waiting for transfers between devices: 6.34 us -> 7.11 us
  starting transfers between devices: 16.6 us -> 16.3 us
    squeeze x1, local copies, waits for them, and re-layouts: 0.88 us -> 0.01 us  [per_device(): own = [green[:, f] for f in range(freqs)]]
    ppermute x14 -> x11, waiting for transfers between devices: 6.34 us -> 7.11 us  [swap(): lax.ppermute(a, axis, [(i, i ^ bit) for i in range({'tx': txs, 'cell': ce...]
    ppermute x14 -> x11, starting transfers between devices: 16.6 us -> 16.3 us  [swap(): lax.ppermute(a, axis, [(i, i ^ bit) for i in range({'tx': txs, 'cell': ce...]
  transfers between devices with their start and end apart: 14 -> 11, of which waited for: 5 -> 3; matrix products, arithmetic and copies ran while one was open for 4% -> 4% of each run, Pallas kernels for 6% -> 6%
where the time goes in v6:
time: 27.7 us; the launch traced here: 27.6 us
  starting transfers between devices  16.3 us (59%)
  waiting for transfers between devices  7.11 us (26%)
  Pallas kernels  3.03 us (11%)
  other arithmetic  0.89 us (3%)
    ppermute x11, starting transfers between devices, swap(): lax.ppermute(a, axis, [(i, i ^ bit) for i in range({'tx': txs, 'cell': ce...  16.3 us
    ppermute x11, waiting for transfers between devices, swap(): lax.ppermute(a, axis, [(i, i ^ bit) for i in range({'tx': txs, 'cell': ce...  7.11 us
    pallas_call x1, Pallas kernels, gates_of(): pl.pallas_call(functools.partial(gate_kernel, len(pieces)), out_shape=jax...  1.45 us
    pallas_call x2, Pallas kernels, responses(): pl.pallas_call(functools.partial(response_kernel, freq, offsets, chips),...  1.45 us
    cos x1, other arithmetic, per_device(): jnp.cos(gate_phase)  0.78 us
  transfers between devices with their start and end apart: 11, of which 3 were waited for; matrix products, arithmetic and copies ran while one was open for 4% of the time, Pallas kernels for 6%

profile of v6, /device:TPU:0, one launch (start us, length us, event | category | flops | bytes accessed | tf_op | source)
XLA Modules:
  0.0 27.6 jit_solution(16888822902926436399)
XLA Ops:
  0.0 0.0 copy-start.1
  0.0 4.0 %collective-permute-start = (bf16[2,2,16,1024]{3,2,1,0:T(8,128)(2,1)}, bf16[2,2,16,1024]{3,2,1,0:T(8,128)(2,1)S(1)}, u32[]{:S(2)}, u32[]{:S(2)}) collective-permute-start(bf16[2,2,16,1024]{3,2,1,0:T(8,128)(2,1)} %refs_3_.3), channel_id=1, source_target_pairs={{0,16},{8,24},{16,0},{24,8},{1,17},{9,25},{17,1},{25,9},{2,18},{10... | collective-permute-start | bytes 393224 | tf_op jit(solution)/shard_map/ppermute | solution.py:142
  4.0 1.6 %collective-permute-start.1 = (bf16[2,2,16,1024]{3,2,1,0:T(8,128)(2,1)}, bf16[2,2,16,1024]{3,2,1,0:T(8,128)(2,1)S(1)}, u32[]{:S(2)}, u32[]{:S(2)}) collective-permute-start(bf16[2,2,16,1024]{3,2,1,0:T(8,128)(2,1)} %refs_3_.3), channel_id=1, source_target_pairs={{0,8},{8,0},{16,24},{24,16},{1,9},{9,1},{17,25},{25,17},{2,10},{10... | collective-permute-start | bytes 393224 | tf_op jit(solution)/shard_map/ppermute | solution.py:142
  5.6 0.8 %multiply_cosine_fusion = (f32[64,2,1]{0,1,2:T(2,128)S(1)}, f32[64,2,1]{0,1,2:T(2,128)S(1)}) fusion(f32[64]{0:T(128)} %param.7, f32[2]{0:T(128)} %param.6), kind=kLoop, calls=%fused_computation.18 | loop fusion | flops 256 | bytes 1288 | tf_op jit(solution)/shard_map/cos | solution.py:139
  6.4 0.1 copy.11.weight_ref
  6.5 0.0 copy-start
  6.5 0.1 weights.1.weight_ref
  6.6 0.0 copy-done.1
  6.7 0.1 collective-permute-start.2
  6.8 3.8 %collective-permute-start.6 = (bf16[2,16,1024]{2,1,0:T(8,128)(2,1)S(1)}, bf16[2,16,1024]{2,1,0:T(8,128)(2,1)S(1)}, u32[]{:S(2)}, u32[]{:S(2)}) collective-permute-start(bf16[2,16,1024]{2,1,0:T(8,128)(2,1)S(1)} %get-tuple-element.16), channel_id=1, source_target_pairs={{0,24},{8,16},{16,8},{24,0},{1,25},{9,17},{17,9},{25,1},{2,26},{10... | collective-permute-start | bytes 196616 | tf_op jit(solution)/shard_map/ppermute | solution.py:142
  10.6 3.3 %collective-permute-done.2.refs_2_ = bf16[2,16,1024]{2,1,0:T(8,128)(2,1)S(1)} collective-permute-done((bf16[2,16,1024]{2,1,0:T(8,128)(2,1)S(1)}, bf16[2,16,1024]{2,1,0:T(8,128)(2,1)S(1)}, u32[]{:S(2)}, u32[]{:S(2)}) %collective-permute-start.2) | collective-permute-done | bytes 65568 | tf_op jit(solution)/shard_map/ppermute | solution.py:142
  13.9 0.0 collective-permute-done.refs_0_
  13.9 0.0 collective-permute-done.1.refs_1_
  13.9 0.0 copy-done
  13.9 0.7 %responses.2 = (f32[4,2,8,1024]{3,2,1,0:T(8,128)S(1)}, f32[4,2,8,1024]{3,2,1,0:T(8,128)S(1)}) custom-call(bf16[2,2,16,1024]{3,2,1,0:T(8,128)(2,1)S(1)} %collective-permute-done.refs_0_, bf16[2,2,16,1024]{3,2,1,0:T(8,128)(2,1)S(1)} %collective-permute-done.1.refs_1_, bf16[2,16,1024]{2,1,0:T(8,128)(2,1)S(1)} %collective-permute-done.2.refs_2_, ...), custom_call_target="tpu_custom_call" | custom-call | flops 536870912 | bytes 4194304 | tf_op jit(solution)/shard_map/responses/pallas_call | solution.py:60
  14.7 0.1 collective-permute-start.3
  14.8 0.6 %collective-permute-start.5 = (f32[3,2,8,1024]{3,2,1,0:T(8,128)S(1)}, f32[3,2,8,1024]{3,2,1,0:T(8,128)S(1)}, u32[]{:S(2)}, u32[]{:S(2)}) collective-permute-start(f32[3,2,8,1024]{3,2,1,0:T(8,128)S(1)} %slice.38), channel_id=1, source_target_pairs={{0,1},{1,0},{2,3},{3,2},{4,5},{5,4},{6,7},{7,6},{8,9},{9,8},{10,11... | collective-permute-start | bytes 589832 | tf_op jit(solution)/shard_map/ppermute | solution.py:142
  15.3 0.0 collective-permute-done.6.refs_2_
  15.3 0.7 %responses.3 = (f32[4,2,8,1024]{3,2,1,0:T(8,128)S(1)}, f32[4,2,8,1024]{3,2,1,0:T(8,128)S(1)}) custom-call(bf16[2,2,16,1024]{3,2,1,0:T(8,128)(2,1)S(1)} %collective-permute-done.refs_0_, bf16[2,2,16,1024]{3,2,1,0:T(8,128)(2,1)S(1)} %collective-permute-done.1.refs_1_, bf16[2,16,1024]{2,1,0:T(8,128)(2,1)S(1)} %collective-permute-done.6.refs_2_, ...), custom_call_target="tpu_custom_call" | custom-call | flops 536870912 | bytes 4194304 | tf_op jit(solution)/shard_map/responses/pallas_call | solution.py:60
  16.0 0.1 collective-permute-start.7
  16.1 0.0 collective-permute-done.3
  16.1 2.5 %collective-permute-start.4 = (f32[2,8,1024]{2,1,0:T(8,128)S(1)}, f32[2,8,1024]{2,1,0:T(8,128)S(1)}, u32[]{:S(2)}, u32[]{:S(2)}) collective-permute-start(f32[2,8,1024]{2,1,0:T(8,128)S(1)} %bitcast_add_fusion), channel_id=1, source_target_pairs={{0,6},{1,7},{2,4},{3,5},{4,2},{5,3},{6,0},{7,1},{8,14},{9,15},{10,... | collective-permute-start | bytes 196616 | tf_op jit(solution)/shard_map/ppermute | solution.py:142
  18.7 0.0 collective-permute-done.5
  18.7 0.0 collective-permute-done.7
  18.8 0.6 %collective-permute-start.8 = (f32[4,8,1024]{2,1,0:T(8,128)S(1)}, f32[4,8,1024]{2,1,0:T(8,128)S(1)}, u32[]{:S(2)}, u32[]{:S(2)}) collective-permute-start(f32[4,8,1024]{2,1,0:T(8,128)S(1)} %get-tuple-element.20), channel_id=1, source_target_pairs={{0,2},{1,3},{2,0},{3,1},{4,6},{5,7},{6,4},{7,5},{8,10},{9,11},{10,... | collective-permute-start | bytes 393224 | tf_op jit(solution)/shard_map/ppermute | solution.py:142
  19.4 1.4 %collective-permute-start.9 = (f32[4,8,1024]{2,1,0:T(8,128)S(1)}, f32[4,8,1024]{2,1,0:T(8,128)S(1)}, u32[]{:S(2)}, u32[]{:S(2)}) collective-permute-start(f32[4,8,1024]{2,1,0:T(8,128)S(1)} %get-tuple-element.21), channel_id=1, source_target_pairs={{0,4},{1,5},{2,6},{3,7},{4,0},{5,1},{6,2},{7,3},{8,12},{9,13},{10,... | collective-permute-start | bytes 393224 | tf_op jit(solution)/shard_map/ppermute | solution.py:142
  20.8 1.5 %collective-permute-start.10 = (f32[2,8,1024]{2,1,0:T(8,128)S(1)}, f32[2,8,1024]{2,1,0:T(8,128)S(1)}, u32[]{:S(2)}, u32[]{:S(2)}) collective-permute-start(f32[2,8,1024]{2,1,0:T(8,128)S(1)} %slice_bitcast_fusion), channel_id=1, source_target_pairs={{0,6},{1,7},{2,4},{3,5},{4,2},{5,3},{6,0},{7,1},{8,14},{9,15},{10,... | collective-permute-start | bytes 196616 | tf_op jit(solution)/shard_map/ppermute | solution.py:142
  22.4 0.0 collective-permute-done.4.refs_0_
  22.4 3.7 %collective-permute-done.10.refs_4_ = f32[2,8,1024]{2,1,0:T(8,128)S(1)} collective-permute-done((f32[2,8,1024]{2,1,0:T(8,128)S(1)}, f32[2,8,1024]{2,1,0:T(8,128)S(1)}, u32[]{:S(2)}, u32[]{:S(2)}) %collective-permute-start.10) | collective-permute-done | bytes 65568 | tf_op jit(solution)/shard_map/ppermute | solution.py:142
  26.0 0.0 collective-permute-done.8.refs_1_
  26.0 0.1 collective-permute-done.9.refs_2_
  26.1 1.5 %gates.1 = f32[64,8,1024]{2,1,0:T(8,128)} custom-call(f32[64,4,128]{2,1,0:T(4,128)S(1)} %weights.1.weight_ref, f32[2,8,1024]{2,1,0:T(8,128)S(1)} %collective-permute-done.4.refs_0_, f32[4,8,1024]{2,1,0:T(8,128)S(1)} %collective-permute-done.8.refs_1_, f32[4,8,1024]{2,1,0:T(8,128)S(1)} %collective-permute-done.9.refs_2_, ...), custom_call_target="tpu_custom_call" | custom-call | tf_op jit(solution)/shard_map/gates/pallas_call | solution.py:106
  (11 shorter events, 0.2 us)
Async XLA Ops:
  0.0 6.6 %copy-start.1 = (bf16[2,2,16,1024]{3,2,1,0:T(8,128)(2,1)S(1)}, bf16[2,2,16,1024]{3,2,1,0:T(8,128)(2,1)}, u32[]{:S(2)}) copy-start(bf16[2,2,16,1024]{3,2,1,0:T(8,128)(2,1)} %refs_3_.3) | copy-start | bytes 393220
  0.0 13.9 %collective-permute-start = (bf16[2,2,16,1024]{3,2,1,0:T(8,128)(2,1)}, bf16[2,2,16,1024]{3,2,1,0:T(8,128)(2,1)S(1)}, u32[]{:S(2)}, u32[]{:S(2)}) collective-permute-start(bf16[2,2,16,1024]{3,2,1,0:T(8,128)(2,1)} %refs_3_.3), channel_id=1, source_target_pairs={{0,16},{8,24},{16,0},{24,8},{1,17},{9,25},{17,1},{25,9},{2,18},{10... | collective-permute-start | bytes 393224 | tf_op jit(solution)/shard_map/ppermute | solution.py:142
  4.0 9.9 %collective-permute-start.1 = (bf16[2,2,16,1024]{3,2,1,0:T(8,128)(2,1)}, bf16[2,2,16,1024]{3,2,1,0:T(8,128)(2,1)S(1)}, u32[]{:S(2)}, u32[]{:S(2)}) collective-permute-start(bf16[2,2,16,1024]{3,2,1,0:T(8,128)(2,1)} %refs_3_.3), channel_id=1, source_target_pairs={{0,8},{8,0},{16,24},{24,16},{1,9},{9,1},{17,25},{25,17},{2,10},{10... | collective-permute-start | bytes 393224 | tf_op jit(solution)/shard_map/ppermute | solution.py:142
  6.5 7.4 %copy-start = (bf16[2,2,1024,1024]{3,2,1,0:T(8,128)(2,1)S(1)}, bf16[2,2,1024,1024]{3,2,1,0:T(8,128)(2,1)}, u32[]{:S(2)}) copy-start(bf16[2,2,1024,1024]{3,2,1,0:T(8,128)(2,1)} %refs_4_.3) | copy-start | bytes 25165828
  6.7 7.2 %collective-permute-start.2 = (bf16[2,16,1024]{2,1,0:T(8,128)(2,1)S(1)}, bf16[2,16,1024]{2,1,0:T(8,128)(2,1)S(1)}, u32[]{:S(2)}, u32[]{:S(2)}) collective-permute-start(bf16[2,16,1024]{2,1,0:T(8,128)(2,1)S(1)} %get-tuple-element.13), channel_id=1, source_target_pairs={{0,24},{8,16},{16,8},{24,0},{1,25},{9,17},{17,9},{25,1},{2,26},{10... | collective-permute-start | bytes 196616 | tf_op jit(solution)/shard_map/ppermute | solution.py:142
  6.8 8.6 %collective-permute-start.6 = (bf16[2,16,1024]{2,1,0:T(8,128)(2,1)S(1)}, bf16[2,16,1024]{2,1,0:T(8,128)(2,1)S(1)}, u32[]{:S(2)}, u32[]{:S(2)}) collective-permute-start(bf16[2,16,1024]{2,1,0:T(8,128)(2,1)S(1)} %get-tuple-element.16), channel_id=1, source_target_pairs={{0,24},{8,16},{16,8},{24,0},{1,25},{9,17},{17,9},{25,1},{2,26},{10... | collective-permute-start | bytes 196616 | tf_op jit(solution)/shard_map/ppermute | solution.py:142
  14.7 1.5 %collective-permute-start.3 = (f32[2,8,1024]{2,1,0:T(8,128)S(1)}, f32[2,8,1024]{2,1,0:T(8,128)S(1)}, u32[]{:S(2)}, u32[]{:S(2)}) collective-permute-start(f32[2,8,1024]{2,1,0:T(8,128)S(1)} %slice_bitcast_fusion.1), channel_id=1, source_target_pairs={{0,1},{1,0},{2,3},{3,2},{4,5},{5,4},{6,7},{7,6},{8,9},{9,8},{10,11... | collective-permute-start | bytes 196616 | tf_op jit(solution)/shard_map/ppermute | solution.py:142
  14.8 3.9 %collective-permute-start.5 = (f32[3,2,8,1024]{3,2,1,0:T(8,128)S(1)}, f32[3,2,8,1024]{3,2,1,0:T(8,128)S(1)}, u32[]{:S(2)}, u32[]{:S(2)}) collective-permute-start(f32[3,2,8,1024]{3,2,1,0:T(8,128)S(1)} %slice.38), channel_id=1, source_target_pairs={{0,1},{1,0},{2,3},{3,2},{4,5},{5,4},{6,7},{7,6},{8,9},{9,8},{10,11... | collective-permute-start | bytes 589832 | tf_op jit(solution)/shard_map/ppermute | solution.py:142
  16.0 2.6 %collective-permute-start.7 = (f32[4,2,8,1024]{3,2,1,0:T(8,128)S(1)}, f32[4,2,8,1024]{3,2,1,0:T(8,128)S(1)}, u32[]{:S(2)}, u32[]{:S(2)}) collective-permute-start(f32[4,2,8,1024]{3,2,1,0:T(8,128)S(1)} %get-tuple-element.18), channel_id=1, source_target_pairs={{0,1},{1,0},{2,3},{3,2},{4,5},{5,4},{6,7},{7,6},{8,9},{9,8},{10,11... | collective-permute-start | bytes 786440 | tf_op jit(solution)/shard_map/ppermute | solution.py:142
  16.1 6.2 %collective-permute-start.4 = (f32[2,8,1024]{2,1,0:T(8,128)S(1)}, f32[2,8,1024]{2,1,0:T(8,128)S(1)}, u32[]{:S(2)}, u32[]{:S(2)}) collective-permute-start(f32[2,8,1024]{2,1,0:T(8,128)S(1)} %bitcast_add_fusion), channel_id=1, source_target_pairs={{0,6},{1,7},{2,4},{3,5},{4,2},{5,3},{6,0},{7,1},{8,14},{9,15},{10,... | collective-permute-start | bytes 196616 | tf_op jit(solution)/shard_map/ppermute | solution.py:142
  18.8 7.2 %collective-permute-start.8 = (f32[4,8,1024]{2,1,0:T(8,128)S(1)}, f32[4,8,1024]{2,1,0:T(8,128)S(1)}, u32[]{:S(2)}, u32[]{:S(2)}) collective-permute-start(f32[4,8,1024]{2,1,0:T(8,128)S(1)} %get-tuple-element.20), channel_id=1, source_target_pairs={{0,2},{1,3},{2,0},{3,1},{4,6},{5,7},{6,4},{7,5},{8,10},{9,11},{10,... | collective-permute-start | bytes 393224 | tf_op jit(solution)/shard_map/ppermute | solution.py:142
  19.4 6.7 %collective-permute-start.9 = (f32[4,8,1024]{2,1,0:T(8,128)S(1)}, f32[4,8,1024]{2,1,0:T(8,128)S(1)}, u32[]{:S(2)}, u32[]{:S(2)}) collective-permute-start(f32[4,8,1024]{2,1,0:T(8,128)S(1)} %get-tuple-element.21), channel_id=1, source_target_pairs={{0,4},{1,5},{2,6},{3,7},{4,0},{5,1},{6,2},{7,3},{8,12},{9,13},{10,... | collective-permute-start | bytes 393224 | tf_op jit(solution)/shard_map/ppermute | solution.py:142
  20.8 5.2 %collective-permute-start.10 = (f32[2,8,1024]{2,1,0:T(8,128)S(1)}, f32[2,8,1024]{2,1,0:T(8,128)S(1)}, u32[]{:S(2)}, u32[]{:S(2)}) collective-permute-start(f32[2,8,1024]{2,1,0:T(8,128)S(1)} %slice_bitcast_fusion), channel_id=1, source_target_pairs={{0,6},{1,7},{2,4},{3,5},{4,2},{5,3},{6,0},{7,1},{8,14},{9,15},{10,... | collective-permute-start | bytes 196616 | tf_op jit(solution)/shard_map/ppermute | solution.py:142
